TPU v7x, 1024 devices: a whole 4x4x32 slice. The times are simulated.
1024 devices in a mesh: pipe: 32 (over z), ctx: 32 (over y, x, core).
Axes of the slice: x: 4, y: 4, z: 32, core: 2. Of those that a mesh axis runs over, the one named last changes fastest.
Arguments:
- segment: bfloat16 [32, 4096, 4096], P('pipe', 'ctx'), may hold values from -6 to 6
- cotangent: bfloat16 [32, 4096, 4096], P('pipe', 'ctx'), may hold values from -6 to 6
- domain: int32 [32, 4096], P('pipe', 'ctx'), may hold values from 0 to 7
- short_filters: float32 [32, 3, 7, 4096], P('pipe'), may hold values from -2.5 to 2.5
- medium_filters: float32 [32, 256, 128], P('pipe'), may hold values from -0.5 to 0.5
Outputs:
- passed_grad: bfloat16 [32, 4096, 4096], P('pipe', 'ctx')
All inputs are finite; a program needn't handle non-finite values.
Results may differ from a plain program's by a relative error of at most 0.0064.
Values may be sent and summed in bfloat16 or wider, within the bound.
No kernel may reach another device: no remote copies, remote signals or barrier semaphores. Data moves between devices by JAX's collectives and lax.ppermute only.
A program may use at most 64 MiB of HBM per device.

v0:
```python
import jax
import jax.numpy as jnp
import numpy as np
from jax import lax
from jax.sharding import PartitionSpec as P

SHORT = 7
MEDIUM = 128
DOMAINS = 8
GSIZE = 16


loss_table = [0.5, 1.0, 1.5, 2.0, 3.0, 0.25, 1.25, 2.5]


def shifted(value, axis, by):
    devices = lax.axis_size(axis)
    pairs = [(i, i + by) for i in range(devices) if 0 <= i + by < devices]
    return lax.ppermute(value, axis, pairs)


def shifted_2(value, axis, steps):
    count = lax.axis_size(axis)
    pairs = [(source, (source + steps) % count) for source in range(count)]
    return lax.ppermute(value, axis, pairs)


def short_causal(padded, taps_short, tok_count):
    total = jnp.zeros((tok_count, padded.shape[1]), jnp.float32)
    for offset in range(SHORT):
        start = SHORT - 1 - offset
        total = total + taps_short[offset] * padded[start : start + tok_count]
    return total


def short_anticausal(padded, taps_short, tok_count):
    total = jnp.zeros((tok_count, padded.shape[1]), jnp.float32)
    for offset in range(SHORT):
        total = total + taps_short[offset] * padded[offset : offset + tok_count]
    return total


def toeplitz_pair(filters):
    lag_near = np.arange(MEDIUM)[:, None] - np.arange(MEDIUM)[None, :]
    lag_far = lag_near + MEDIUM
    near = jnp.take(filters, np.clip(lag_near, 0, MEDIUM - 1), axis=1)
    far = jnp.take(filters, np.clip(lag_far, 0, MEDIUM - 1), axis=1)
    near = jnp.where(jnp.asarray(lag_near >= 0)[None], near, jnp.zeros_like(near))
    far = jnp.where(jnp.asarray(lag_far <= MEDIUM - 1)[None], far, jnp.zeros_like(far))
    return (near, far)


def medium_causal(signal, before, near, far):
    group_count = near.shape[0]
    tok_count = signal.shape[0]
    width = signal.shape[1]
    full = jnp.concatenate([before, signal], 0).T
    columns = full.reshape(group_count, GSIZE, tok_count // MEDIUM + 1, MEDIUM)
    windows = jnp.concatenate([columns[:, :, :-1], columns[:, :, 1:]], 3)
    joined = jnp.concatenate([far, near], 2)
    out = jnp.einsum("gts,gcbs->gcbt", joined, windows, preferred_element_type=jnp.float32)
    return out.reshape(width, tok_count).T.astype(jnp.bfloat16)


def medium_anticausal(signal, after, near, far):
    group_count = near.shape[0]
    tok_count = signal.shape[0]
    width = signal.shape[1]
    full = jnp.concatenate([signal, after], 0).T
    columns = full.reshape(group_count, GSIZE, tok_count // MEDIUM + 1, MEDIUM)
    windows = jnp.concatenate([columns[:, :, :-1], columns[:, :, 1:]], 3)
    joined = jnp.concatenate([near, far], 1)
    out = jnp.einsum("gts,gcbt->gcbs", joined, windows, preferred_element_type=jnp.float32)
    return out.reshape(width, tok_count).T.astype(jnp.bfloat16)


def body(segment, cotangent, domain, short_filters, medium_filters):
    feats = segment[0]
    grads = cotangent[0]
    domain_ids = domain[0]
    taps_short = short_filters[0]
    taps_medium = medium_filters[0].astype(jnp.bfloat16)
    tok_count = feats.shape[0]
    rim = SHORT - 1
    prior = shifted(feats[tok_count - rim :], "ctx", 1)
    padded = jnp.concatenate([prior, feats], 0).astype(jnp.float32)
    q_stream = short_causal(padded, taps_short[0], tok_count)
    k_stream = short_causal(padded, taps_short[1], tok_count)
    v_stream = short_causal(padded, taps_short[2], tok_count)
    mixed = (k_stream * v_stream).astype(jnp.bfloat16)
    onehot = domain_ids[:, None] == jnp.arange(DOMAINS, dtype=jnp.int32)[None, :]
    table = jnp.asarray(loss_table, jnp.float32)
    token_weight = jnp.sum(jnp.where(onehot, table[None, :], jnp.zeros((), jnp.float32)), axis=1)
    gated = grads.astype(jnp.float32) * token_weight[:, None]
    conv_grad = (q_stream * gated).astype(jnp.bfloat16)
    ctx_count = lax.axis_size("ctx")
    local_groups = taps_medium.shape[0] // ctx_count
    first_group = lax.axis_index("ctx") * local_groups
    local_taps = lax.dynamic_slice_in_dim(taps_medium, first_group, local_groups, 0)
    near, far = toeplitz_pair(local_taps)
    mixed_ch, grad_ch = (
        lax.all_to_all(mixed, "ctx", split_axis=1, concat_axis=0, tiled=True),
        lax.all_to_all(conv_grad, "ctx", split_axis=1, concat_axis=0, tiled=True),
    )
    blank = jnp.zeros((MEDIUM, mixed_ch.shape[1]), jnp.bfloat16)
    out_ch = medium_causal(mixed_ch, blank, near, far)
    back_ch = medium_anticausal(grad_ch, blank, near, far)
    conv_out, mixed_grad = (
        lax.all_to_all(out_ch, "ctx", split_axis=0, concat_axis=1, tiled=True),
        lax.all_to_all(back_ch, "ctx", split_axis=0, concat_axis=1, tiled=True),
    )
    mixed_f = mixed_grad.astype(jnp.float32)
    grad_query = gated * conv_out.astype(jnp.float32)
    grad_key = mixed_f * v_stream
    grad_value = mixed_f * k_stream
    next_query, next_key, next_value = (
        shifted(grad_query[:rim].astype(jnp.bfloat16), "ctx", -1).astype(jnp.float32),
        shifted(grad_key[:rim].astype(jnp.bfloat16), "ctx", -1).astype(jnp.float32),
        shifted(grad_value[:rim].astype(jnp.bfloat16), "ctx", -1).astype(jnp.float32),
    )
    total = short_anticausal(jnp.concatenate([grad_query, next_query], 0), taps_short[0], tok_count)
    total = total + short_anticausal(
        jnp.concatenate([grad_key, next_key], 0), taps_short[1], tok_count
    )
    total = total + short_anticausal(
        jnp.concatenate([grad_value, next_value], 0), taps_short[2], tok_count
    )
    input_grad = total.astype(jnp.bfloat16)
    received = shifted_2(input_grad, "pipe", -1)
    return received[None]


def solution(mesh):
    placed = (
        P("pipe", "ctx", None),
        P("pipe", "ctx", None),
        P("pipe", "ctx"),
        P("pipe", None, None, None),
        P("pipe", None, None),
    )
    return jax.shard_map(
        body, mesh=mesh, in_specs=placed, out_specs=P("pipe", "ctx", None), check_vma=False
    )
```

profile of v0, /device:TPU:24, one launch (start us, length us, event | category | flops | bytes accessed | tf_op | source)
XLA Modules:
  0.0 353.9 jit_solution(9303880573088014830)
XLA Ops:
  0.9 1.9 collective-permute-start
  4.0 1.6 copy.69
  5.7 2.9 collective-permute-done
  10.0 13.6 %multiply_convert_fusion = (bf16[128,4096]{0,1:T(8,128)(2,1)S(1)}, f32[128,4096]{0,1:T(8,128)}, f32[128,4096]{0,1:T(8,128)}) fusion(f32[134,4096]{0,1:T(8,128)S(1)} %maximum_convert_fusion, f32[4096]{0:T(1024)S(1)} %bitcast.112, f32[4096]{0:T(1024)S(1)} %bitcast.114, f32[4096]{0:T(1024)S(1)} %bitcast.116, f32[4096]{0:T(1024)S(1)} %bitcast.118, ...), kind=kLoop, calls=%fused_computation.107 | loop fusion | flops 14680064 | bytes 20152320 | tf_op jit(solution)/shard_map/convert_element_type | solution.py:90
  23.6 1.3 copy.71
  24.9 13.1 %all-to-all-start = ((bf16[128,32,128]{2,0,1:T(8,128)(2,1)}), bf16[128,32,128]{2,0,1:T(8,128)(2,1)S(1)}, u32[]{:S(2)}, u32[]{:S(2)}) async-start(bf16[128,32,128]{2,0,1:T(8,128)(2,1)} %copy.71), calls=%async_computation | async-start | bytes 2097152 | tf_op jit(solution)/shard_map/all_to_all | solution.py:102
  38.1 57.8 %gather_fusion.1 = bf16[16384,8]{1,0:T(8,128)(2,1)} fusion(bf16[8,128]{0,1:T(8,128)(2,1)S(1)} %bitcast.88, s32[16384]{0:T(1024)S(1)} %broadcast_clamp_fusion), kind=kCustom, calls=%fused_computation.1.clone | custom fusion | bytes 589824 | tf_op jit(solution)/shard_map/jit(_take)/gather | solution.py:46
  95.9 3.6 %copy.92 = bf16[128,128,8]{1,0,2:T(8,128)(2,1)S(1)} copy(bf16[128,128,8]{2,1,0:T(8,128)(2,1)} %bitcast.91) | data formatting | bytes 524288 | tf_op jit(solution)/shard_map/jit(_take)/gather | solution.py:46
  99.6 57.8 %gather_fusion = bf16[16384,8]{1,0:T(8,128)(2,1)} fusion(bf16[8,128]{0,1:T(8,128)(2,1)S(1)} %bitcast.89, s32[16384]{0:T(1024)S(1)} %broadcast_clamp_fusion.1), kind=kCustom, calls=%fused_computation.clone | custom fusion | bytes 589824 | tf_op jit(solution)/shard_map/jit(_take)/gather | solution.py:47
  157.4 3.6 %copy.91 = bf16[128,128,8]{1,0,2:T(8,128)(2,1)S(1)} copy(bf16[128,128,8]{2,1,0:T(8,128)(2,1)} %bitcast.90) | data formatting | bytes 524288 | tf_op jit(solution)/shard_map/jit(_take)/gather | solution.py:47
  166.6 7.5 %all-to-all-start.1 = ((bf16[32,128,128]{2,1,0:T(8,128)(2,1)}), bf16[32,128,128]{2,1,0:T(8,128)(2,1)S(1)}, u32[]{:S(2)}, u32[]{:S(2)}) async-start(bf16[32,128,128]{2,1,0:T(8,128)(2,1)} %bitcast.31), calls=%async_computation.1 | async-start | bytes 2097152 | tf_op jit(solution)/shard_map/all_to_all | solution.py:109
  175.7 13.4 %all-to-all-done.1 = bf16[32,128,128]{2,1,0:T(8,128)(2,1)S(1)} async-done(((bf16[32,128,128]{2,1,0:T(8,128)(2,1)}), bf16[32,128,128]{2,1,0:T(8,128)(2,1)S(1)}, u32[]{:S(2)}, u32[]{:S(2)}) %all-to-all-start.1) | async-done | bytes 1048608 | tf_op jit(solution)/shard_map/all_to_all | solution.py:109
  190.4 16.0 %bitcast_multiply_fusion = (f32[128,4096]{0,1:T(8,128)S(1)}, bf16[128,4096]{0,1:T(8,128)(2,1)}) fusion(bf16[1,128,4096]{1,2,0:T(8,128)(2,1)S(1)} %copy.68, f32[128]{0:T(128)S(1)} %select_reduce_fusion, bf16[32,128,128]{1,2,0:T(8,128)(2,1)} %copy.77, f32[134,4096]{0,1:T(8,128)} %copy-done.2, f32[4096]{0:T(1024)S(1)} %bitcast.142, f32[4096]{0:T(1024)S(1)} %bitcast.140, ...), kind=kLoop, calls=%fused_computation.101 | loop fusion | flops 9961472 | bytes 20038144 | tf_op jit(solution)/shard_map/mul | solution.py:113
  206.4 1.6 copy.80
  208.0 20.9 %all_to_all.64 = bf16[128,32,128]{2,0,1:T(8,128)(2,1)} all-to-all(bf16[128,32,128]{2,0,1:T(8,128)(2,1)S(1)} %copy.80), channel_id=1, replica_groups=mesh['pipe'=32,'ctx'=32] {'ctx'}, dimensions={1} | all-to-all | bytes 2097152 | tf_op jit(solution)/shard_map/all_to_all | solution.py:103
  228.9 1.5 copy.81
  231.5 1.6 reshape.90
  236.6 6.8 %all-to-all-start.3 = ((bf16[32,128,128]{2,1,0:T(8,128)(2,1)}), bf16[32,128,128]{2,1,0:T(8,128)(2,1)}, u32[]{:S(2)}, u32[]{:S(2)}) async-start(bf16[32,128,128]{2,1,0:T(8,128)(2,1)} %bitcast.47), calls=%async_computation.3 | async-start | bytes 2097152 | tf_op jit(solution)/shard_map/all_to_all | solution.py:110
  244.0 4.6 %collective-permute-start.1 = (bf16[6,4096]{1,0:T(8,128)(2,1)S(1)}, bf16[6,4096]{1,0:T(8,128)(2,1)S(1)}, u32[]{:S(2)}, u32[]{:S(2)}) collective-permute-start(bf16[6,4096]{1,0:T(8,128)(2,1)S(1)} %copy.78), channel_id=1, source_target_pairs={{1,0},{2,1},{3,2},{4,3},{5,4},{6,5},{7,6},{8,7},{9,8},{10,9},{11,1... | collective-permute-start | bytes 147464 | tf_op jit(solution)/shard_map/ppermute | solution.py:19
  248.6 9.9 %all-to-all-done.3 = bf16[32,128,128]{2,1,0:T(8,128)(2,1)} async-done(((bf16[32,128,128]{2,1,0:T(8,128)(2,1)}), bf16[32,128,128]{2,1,0:T(8,128)(2,1)}, u32[]{:S(2)}, u32[]{:S(2)}) %all-to-all-start.3) | async-done | bytes 1048608 | tf_op jit(solution)/shard_map/all_to_all | solution.py:110
  258.5 1.6 copy.83
  260.1 2.5 bitcast_multiply_fusion.2
  262.7 1.3 copy-done.3
  265.7 1.6 copy.86
  267.3 3.0 collective-permute-start.3
  270.7 2.9 collective-permute-start.2
  273.7 1.7 copy.79
  275.6 1.8 copy.87
  277.3 1.8 copy.85
  279.3 40.2 %fusion.5 = bf16[128,4096]{0,1:T(8,128)(2,1)S(1)} fusion(f32[128,4096]{0,1:T(8,128)} %copy-done.4, f32[6,4096]{0,1:T(8,128)} %copy.87, f32[128,4096]{0,1:T(8,128)} %copy-done.3, f32[6,4096]{0,1:T(8,128)} %copy.85, f32[128,4096]{0,1:T(8,128)S(1)} %get-tuple-element.13, f32[6,4096]{0,1:T(8,128)} %copy.79, f32[4096]{0:T(1024)S(1)} %bitcast.143, ...), kind=kLoop, calls=%fused_computation.37 | loop fusion | flops 31457280 | bytes 7979008 | tf_op jit(solution)/shard_map/convert_element_type | solution.py:128
  319.5 11.0 %collective-permute-start.4 = (bf16[128,4096]{0,1:T(8,128)(2,1)S(1)}, bf16[128,4096]{0,1:T(8,128)(2,1)S(1)}, u32[]{:S(2)}, u32[]{:S(2)}) collective-permute-start(bf16[128,4096]{0,1:T(8,128)(2,1)S(1)} %fusion.5), channel_id=1, source_target_pairs={{0,992},{32,0},{64,32},{96,64},{128,96},{160,128},{192,160},{224,1... | collective-permute-start | bytes 3145736 | tf_op jit(solution)/shard_map/ppermute | solution.py:25
  330.5 22.0 %collective-permute-done.4 = bf16[128,4096]{0,1:T(8,128)(2,1)S(1)} collective-permute-done((bf16[128,4096]{0,1:T(8,128)(2,1)S(1)}, bf16[128,4096]{0,1:T(8,128)(2,1)S(1)}, u32[]{:S(2)}, u32[]{:S(2)}) %collective-permute-start.4) | collective-permute-done | bytes 1048608 | tf_op jit(solution)/shard_map/ppermute | solution.py:25
  (146 shorter events, 20.3 us)
Async XLA Ops:
  0.9 7.7 %collective-permute-start = (bf16[6,4096]{1,0:T(8,128)(2,1)S(1)}, bf16[6,4096]{1,0:T(8,128)(2,1)S(1)}, u32[]{:S(2)}, u32[]{:S(2)}) collective-permute-start(bf16[6,4096]{1,0:T(8,128)(2,1)S(1)} %slice_bitcast_fusion), channel_id=1, source_target_pairs={{0,1},{1,2},{2,3},{3,4},{4,5},{5,6},{6,7},{7,8},{8,9},{9,10},{10,1... | collective-permute-start | bytes 147464 | tf_op jit(solution)/shard_map/ppermute | solution.py:19
  3.8 6.1 %copy-start.18 = (f32[1,1,1,4096]{3,0,2,1:T(1,128)}, f32[1,1,1,4096]{3,0,2,1:T(1,128)S(1)}, u32[]{:S(2)}) copy-start(f32[1,1,1,4096]{3,0,2,1:T(1,128)S(1)} %get-tuple-element.22) | copy-start | bytes 49156
  3.8 6.1 %copy-start.20 = (f32[1,1,1,4096]{3,0,2,1:T(1,128)}, f32[1,1,1,4096]{3,0,2,1:T(1,128)S(1)}, u32[]{:S(2)}) copy-start(f32[1,1,1,4096]{3,0,2,1:T(1,128)S(1)} %get-tuple-element.23) | copy-start | bytes 49156
  3.8 6.1 %copy-start.22 = (f32[1,1,1,4096]{3,0,2,1:T(1,128)}, f32[1,1,1,4096]{3,0,2,1:T(1,128)S(1)}, u32[]{:S(2)}) copy-start(f32[1,1,1,4096]{3,0,2,1:T(1,128)S(1)} %get-tuple-element.24) | copy-start | bytes 49156
  3.8 6.1 %copy-start.24 = (f32[1,1,1,4096]{3,0,2,1:T(1,128)}, f32[1,1,1,4096]{3,0,2,1:T(1,128)S(1)}, u32[]{:S(2)}) copy-start(f32[1,1,1,4096]{3,0,2,1:T(1,128)S(1)} %get-tuple-element.25) | copy-start | bytes 49156
  3.8 6.1 %copy-start.26 = (f32[1,1,1,4096]{3,0,2,1:T(1,128)}, f32[1,1,1,4096]{3,0,2,1:T(1,128)S(1)}, u32[]{:S(2)}) copy-start(f32[1,1,1,4096]{3,0,2,1:T(1,128)S(1)} %get-tuple-element.26) | copy-start | bytes 49156
  3.8 6.1 %copy-start.28 = (f32[1,1,1,4096]{3,0,2,1:T(1,128)}, f32[1,1,1,4096]{3,0,2,1:T(1,128)S(1)}, u32[]{:S(2)}) copy-start(f32[1,1,1,4096]{3,0,2,1:T(1,128)S(1)} %get-tuple-element.27) | copy-start | bytes 49156
  3.8 6.1 %copy-start.30 = (f32[1,1,1,4096]{3,0,2,1:T(1,128)}, f32[1,1,1,4096]{3,0,2,1:T(1,128)S(1)}, u32[]{:S(2)}) copy-start(f32[1,1,1,4096]{3,0,2,1:T(1,128)S(1)} %get-tuple-element.28) | copy-start | bytes 49156
  3.8 6.1 %copy-start.32 = (f32[1,1,1,4096]{3,0,2,1:T(1,128)}, f32[1,1,1,4096]{3,0,2,1:T(1,128)S(1)}, u32[]{:S(2)}) copy-start(f32[1,1,1,4096]{3,0,2,1:T(1,128)S(1)} %get-tuple-element.29) | copy-start | bytes 49156
  3.9 6.1 %copy-start.34 = (f32[1,1,1,4096]{3,0,2,1:T(1,128)}, f32[1,1,1,4096]{3,0,2,1:T(1,128)S(1)}, u32[]{:S(2)}) copy-start(f32[1,1,1,4096]{3,0,2,1:T(1,128)S(1)} %get-tuple-element.30) | copy-start | bytes 49156
  3.9 6.1 %copy-start.36 = (f32[1,1,1,4096]{3,0,2,1:T(1,128)}, f32[1,1,1,4096]{3,0,2,1:T(1,128)S(1)}, u32[]{:S(2)}) copy-start(f32[1,1,1,4096]{3,0,2,1:T(1,128)S(1)} %get-tuple-element.31) | copy-start | bytes 49156
  3.9 6.1 %copy-start.38 = (f32[1,1,1,4096]{3,0,2,1:T(1,128)}, f32[1,1,1,4096]{3,0,2,1:T(1,128)S(1)}, u32[]{:S(2)}) copy-start(f32[1,1,1,4096]{3,0,2,1:T(1,128)S(1)} %get-tuple-element.32) | copy-start | bytes 49156
  3.9 6.1 %copy-start.40 = (f32[1,1,1,4096]{3,0,2,1:T(1,128)}, f32[1,1,1,4096]{3,0,2,1:T(1,128)S(1)}, u32[]{:S(2)}) copy-start(f32[1,1,1,4096]{3,0,2,1:T(1,128)S(1)} %get-tuple-element.33) | copy-start | bytes 49156
  3.9 186.5 %copy-start.10 = (f32[1,1,1,4096]{3,0,2,1:T(1,128)}, f32[1,1,1,4096]{3,0,2,1:T(1,128)S(1)}, u32[]{:S(2)}) copy-start(f32[1,1,1,4096]{3,0,2,1:T(1,128)S(1)} %get-tuple-element.18) | copy-start | bytes 49156
  3.9 186.5 %copy-start.12 = (f32[1,1,1,4096]{3,0,2,1:T(1,128)}, f32[1,1,1,4096]{3,0,2,1:T(1,128)S(1)}, u32[]{:S(2)}) copy-start(f32[1,1,1,4096]{3,0,2,1:T(1,128)S(1)} %get-tuple-element.19) | copy-start | bytes 49156
  3.9 186.5 %copy-start.14 = (f32[1,1,1,4096]{3,0,2,1:T(1,128)}, f32[1,1,1,4096]{3,0,2,1:T(1,128)S(1)}, u32[]{:S(2)}) copy-start(f32[1,1,1,4096]{3,0,2,1:T(1,128)S(1)} %get-tuple-element.20) | copy-start | bytes 49156
  3.9 186.5 %copy-start.16 = (f32[1,1,1,4096]{3,0,2,1:T(1,128)}, f32[1,1,1,4096]{3,0,2,1:T(1,128)S(1)}, u32[]{:S(2)}) copy-start(f32[1,1,1,4096]{3,0,2,1:T(1,128)S(1)} %get-tuple-element.21) | copy-start | bytes 49156
  9.9 13.7 %copy-start.2 = (f32[134,4096]{0,1:T(8,128)}, f32[134,4096]{0,1:T(8,128)S(1)}, u32[]{:S(2)}) copy-start(f32[134,4096]{0,1:T(8,128)S(1)} %maximum_convert_fusion) | copy-start | bytes 6586372
  23.6 14.4 %copy-start.51 = (s32[16384]{0:T(1024)S(1)}, s32[16384]{0:T(1024)}, u32[]{:S(2)}) copy-start(s32[16384]{0:T(1024)} %constant.69) | copy-start | bytes 196612
  24.9 137.0 %all-to-all-start = ((bf16[128,32,128]{2,0,1:T(8,128)(2,1)}), bf16[128,32,128]{2,0,1:T(8,128)(2,1)S(1)}, u32[]{:S(2)}, u32[]{:S(2)}) async-start(bf16[128,32,128]{2,0,1:T(8,128)(2,1)} %copy.71), calls=%async_computation | async-start | bytes 2097152 | tf_op jit(solution)/shard_map/all_to_all | solution.py:102
  165.3 8.8 %copy-start.5 = (bf16[1,128,4096]{2,1,0:T(8,128)(2,1)S(1)}, bf16[1,128,4096]{2,1,0:T(8,128)(2,1)}, u32[]{:S(2)}) copy-start(bf16[1,128,4096]{2,1,0:T(8,128)(2,1)} %param.13) | copy-start | bytes 3145732
  166.6 8.2 %copy-start.54 = (s32[1,128]{1,0:T(1,128)S(1)}, s32[1,128]{1,0:T(1,128)}, u32[]{:S(2)}) copy-start(s32[1,128]{1,0:T(1,128)} %param.14) | copy-start | bytes 1540
  166.6 8.2 %copy-start.55 = (f32[8]{0:T(128)S(1)}, f32[8]{0:T(128)}, u32[]{:S(2)}) copy-start(f32[8]{0:T(128)} %constant.13.clone) | copy-start | bytes 100
  166.6 22.5 %all-to-all-start.1 = ((bf16[32,128,128]{2,1,0:T(8,128)(2,1)}), bf16[32,128,128]{2,1,0:T(8,128)(2,1)S(1)}, u32[]{:S(2)}, u32[]{:S(2)}) async-start(bf16[32,128,128]{2,1,0:T(8,128)(2,1)} %bitcast.31), calls=%async_computation.1 | async-start | bytes 2097152 | tf_op jit(solution)/shard_map/all_to_all | solution.py:109
  175.7 30.7 %copy-start.46 = (f32[1,1,1,4096]{3,0,2,1:T(1,128)}, f32[1,1,1,4096]{3,0,2,1:T(1,128)S(1)}, u32[]{:S(2)}) copy-start(f32[1,1,1,4096]{3,0,2,1:T(1,128)S(1)} %get-tuple-element.36) | copy-start | bytes 49156
  175.7 30.7 %copy-start.48 = (f32[1,1,1,4096]{3,0,2,1:T(1,128)}, f32[1,1,1,4096]{3,0,2,1:T(1,128)S(1)}, u32[]{:S(2)}) copy-start(f32[1,1,1,4096]{3,0,2,1:T(1,128)S(1)} %get-tuple-element.37) | copy-start | bytes 49156
  236.6 21.9 %all-to-all-start.3 = ((bf16[32,128,128]{2,1,0:T(8,128)(2,1)}), bf16[32,128,128]{2,1,0:T(8,128)(2,1)}, u32[]{:S(2)}, u32[]{:S(2)}) async-start(bf16[32,128,128]{2,1,0:T(8,128)(2,1)} %bitcast.47), calls=%async_computation.3 | async-start | bytes 2097152 | tf_op jit(solution)/shard_map/all_to_all | solution.py:110
  244.0 29.7 %collective-permute-start.1 = (bf16[6,4096]{1,0:T(8,128)(2,1)S(1)}, bf16[6,4096]{1,0:T(8,128)(2,1)S(1)}, u32[]{:S(2)}, u32[]{:S(2)}) collective-permute-start(bf16[6,4096]{1,0:T(8,128)(2,1)S(1)} %copy.78), channel_id=1, source_target_pairs={{1,0},{2,1},{3,2},{4,3},{5,4},{6,5},{7,6},{8,7},{9,8},{10,9},{11,1... | collective-permute-start | bytes 147464 | tf_op jit(solution)/shard_map/ppermute | solution.py:19
  267.3 8.3 %collective-permute-start.3 = (bf16[6,4096]{1,0:T(8,128)(2,1)S(1)}, bf16[6,4096]{1,0:T(8,128)(2,1)S(1)}, u32[]{:S(2)}, u32[]{:S(2)}) collective-permute-start(bf16[6,4096]{1,0:T(8,128)(2,1)S(1)} %copy.86), channel_id=1, source_target_pairs={{1,0},{2,1},{3,2},{4,3},{5,4},{6,5},{7,6},{8,7},{9,8},{10,9},{11,1... | collective-permute-start | bytes 147464 | tf_op jit(solution)/shard_map/ppermute | solution.py:19
  270.7 6.6 %collective-permute-start.2 = (bf16[6,4096]{1,0:T(8,128)(2,1)S(1)}, bf16[6,4096]{1,0:T(8,128)(2,1)S(1)}, u32[]{:S(2)}, u32[]{:S(2)}) collective-permute-start(bf16[6,4096]{1,0:T(8,128)(2,1)S(1)} %copy.84), channel_id=1, source_target_pairs={{1,0},{2,1},{3,2},{4,3},{5,4},{6,5},{7,6},{8,7},{9,8},{10,9},{11,1... | collective-permute-start | bytes 147464 | tf_op jit(solution)/shard_map/ppermute | solution.py:19
  279.3 74.5 %copy-start.1 = (f32[1,256,128]{2,1,0:T(8,128)S(1)}, f32[1,256,128]{2,1,0:T(8,128)}, u32[]{:S(2)}) copy-start(f32[1,256,128]{2,1,0:T(8,128)} %param.16) | copy-start | bytes 393220
  319.5 33.0 %collective-permute-start.4 = (bf16[128,4096]{0,1:T(8,128)(2,1)S(1)}, bf16[128,4096]{0,1:T(8,128)(2,1)S(1)}, u32[]{:S(2)}, u32[]{:S(2)}) collective-permute-start(bf16[128,4096]{0,1:T(8,128)(2,1)S(1)} %fusion.5), channel_id=1, source_target_pairs={{0,992},{32,0},{64,32},{96,64},{128,96},{160,128},{192,160},{224,1... | collective-permute-start | bytes 3145736 | tf_op jit(solution)/shard_map/ppermute | solution.py:25
  (32 other events, 109.8 us)
where the time goes:
time: 357 us; the launch traced here: 354 us
  local copies, waits for them, and re-layouts  157 us (44%)
  other arithmetic  74 us (21%)
  starting transfers between devices  50.9 us (14%)
  waiting for transfers between devices  48.3 us (14%)
  blocking collectives  20.9 us (6%)
    gather x2, local copies, waits for them, and re-layouts, toeplitz_pair(): far = jnp.take(filters, np.clip(lag_far, 0, MEDIUM - 1), axis=1)  61.4 us
    gather x2, local copies, waits for them, and re-layouts, toeplitz_pair(): near = jnp.take(filters, np.clip(lag_near, 0, MEDIUM - 1), axis=1)  61.4 us
    convert_element_type x1, other arithmetic, body(): input_grad = total.astype(jnp.bfloat16)  40.2 us
    ppermute x1, waiting for transfers between devices, shifted_2(): return lax.ppermute(value, axis, pairs)  22 us
    all_to_all x1, blocking collectives, body(): lax.all_to_all(conv_grad, 'ctx', split_axis=1, concat_axis=0, tiled=True)  20.9 us
    mul x1, other arithmetic, body(): grad_query = gated * conv_out.astype(jnp.float32)  16 us
    convert_element_type x1, other arithmetic, body(): mixed = (k_stream * v_stream).astype(jnp.bfloat16)  13.6 us
    all_to_all x1, waiting for transfers between devices, body(): lax.all_to_all(out_ch, 'ctx', split_axis=0, concat_axis=1, tiled=True)  13.4 us
  transfers between devices with their start and end apart: 8, of which 4 were waited for; matrix products, arithmetic and copies ran while one was open for 39% of the time, Pallas kernels for 0%

commit v1 on v0

v1 whole, which is shorter than its diff:
```python
import functools

import jax
import jax.numpy as jnp
from jax import lax
from jax.experimental import pallas as pl
from jax.experimental.pallas import tpu as pltpu
from jax.sharding import PartitionSpec as P

SHORT = 7
MEDIUM = 128
GSIZE = 16
LANES = 128
RIM = 8
WIDTH = 256

loss_table = [0.5, 1.0, 1.5, 2.0, 3.0, 0.25, 1.25, 2.5]

HALO_PARTS = (4, 12)
PASS_PARTS = (4, 4, 4, 4)


def ring_pairs(count, by):
    return [(i, i + by) for i in range(count) if 0 <= i + by < count]


def token_weights(domain_ref):
    ids = domain_ref[...]
    row = jnp.zeros(ids.shape, jnp.float32)
    for index, value in enumerate(loss_table):
        row = jnp.where(ids == index, jnp.float32(value), row)
    return jnp.broadcast_to(row, (MEDIUM, MEDIUM)).T


def reversal():
    rows = lax.broadcasted_iota(jnp.int32, (MEDIUM, MEDIUM), 0)
    cols = lax.broadcasted_iota(jnp.int32, (MEDIUM, MEDIUM), 1)
    return (rows + cols == MEDIUM - 1).astype(jnp.float32).astype(jnp.bfloat16)


def identity():
    rows = lax.broadcasted_iota(jnp.int32, (MEDIUM, MEDIUM), 0)
    cols = lax.broadcasted_iota(jnp.int32, (MEDIUM, MEDIUM), 1)
    return (rows == cols).astype(jnp.float32).astype(jnp.bfloat16)


def streams_kernel(seg_ref, rim_ref, cot_ref, domain_ref, short_ref, k_ref, v_ref, mixed_ref, grad_ref):
    weight = token_weights(domain_ref)
    flip = reversal()
    for lane in range(0, seg_ref.shape[2], LANES):
        cols = pl.ds(lane, LANES)
        x = jnp.concatenate(
            [rim_ref[:, cols].astype(jnp.float32), seg_ref[0, :, cols].astype(jnp.float32)], 0
        )
        sums = [None, None, None]
        for j in range(SHORT):
            moved = (x if j == 0 else pltpu.roll(x, j, 0))[RIM:]
            for i in range(3):
                term = short_ref[0, i, j, cols][None, :] * moved
                sums[i] = term if j == 0 else sums[i] + term
        q, k, v = sums
        k_ref[:, cols] = k.astype(jnp.bfloat16)
        v_ref[:, cols] = v.astype(jnp.bfloat16)
        mixed_ref[pl.ds(lane, LANES), :] = (k * v).T.astype(jnp.bfloat16)
        gated = cot_ref[0, :, cols].astype(jnp.float32) * weight
        grad = (q * gated).astype(jnp.bfloat16)
        back = jnp.dot(flip, grad, preferred_element_type=jnp.float32)
        grad_ref[pl.ds(lane, LANES), :] = back.T.astype(jnp.bfloat16)


def grads_kernel(
    taps_ref, mixed_ref, before_ref, grad_ref, after_ref, k_ref, v_ref, cot_ref, domain_ref, short_ref,
    out_ref, own_ref, sent_ref, conv_ref, back_ref,
):
    width = k_ref.shape[1]
    rows = lax.broadcasted_iota(jnp.int32, (MEDIUM, MEDIUM), 0)
    cols = lax.broadcasted_iota(jnp.int32, (MEDIUM, MEDIUM), 1)
    near_mask = cols >= rows
    for g in range(width // GSIZE):
        at = pl.ds(g * GSIZE, GSIZE)
        taps = taps_ref[0, g].astype(jnp.bfloat16).astype(jnp.float32)
        spread = jnp.broadcast_to(taps[None, :], (MEDIUM, MEDIUM))
        circle = pltpu.roll(spread, 0, 1, stride=1, stride_axis=0)
        near = jnp.where(near_mask, circle, 0.0).astype(jnp.bfloat16)
        far = jnp.where(near_mask, 0.0, circle).astype(jnp.bfloat16)
        recent = jnp.concatenate([mixed_ref[at, :], grad_ref[at, :]], 0)
        older = jnp.concatenate([before_ref[at, :], after_ref[at, :]], 0)
        both = jnp.dot(
            jnp.concatenate([older, recent], 1),
            jnp.concatenate([far, near], 0),
            preferred_element_type=jnp.float32,
        ).astype(jnp.bfloat16)
        conv_ref[at, :] = both[:GSIZE]
        back_ref[at, :] = both[GSIZE:]
    weight = token_weights(domain_ref)
    keep, flip = identity(), reversal()
    contract = (((1,), (1,)), ((), ()))
    tail = lax.broadcasted_iota(jnp.int32, (RIM, LANES), 0)
    for lane in range(0, width, LANES):
        at = pl.ds(lane, LANES)
        conv = lax.dot_general(keep, conv_ref[at, :], contract, preferred_element_type=jnp.float32)
        back = lax.dot_general(flip, back_ref[at, :], contract, preferred_element_type=jnp.float32)
        gated = cot_ref[0, :, at].astype(jnp.float32) * weight
        grads = (
            gated * conv,
            back * v_ref[:, at].astype(jnp.float32),
            back * k_ref[:, at].astype(jnp.float32),
        )
        total = own = sent = None
        for j in range(SHORT):
            part = None
            for i in range(3):
                term = short_ref[0, i, j, at][None, :] * grads[i]
                part = term if i == 0 else part + term
            if j == 0:
                total = part
                own = part[MEDIUM - RIM :]
                sent = jnp.zeros_like(own)
                continue
            part = pltpu.roll(part, MEDIUM - j, 0)
            total = total + part
            last = part[MEDIUM - RIM :]
            inside = tail < RIM - j
            own = own + jnp.where(inside, last, 0.0)
            sent = sent + jnp.where(inside, 0.0, last)
        out_ref[:, at] = total[: MEDIUM - RIM].astype(jnp.bfloat16)
        own_ref[:, at] = own
        sent_ref[:, at] = sent


def streams(segment, rim, cotangent, domain, short_filters, start, size):
    first = start // WIDTH
    wide = jax.ShapeDtypeStruct((MEDIUM, size), jnp.bfloat16)
    tall = jax.ShapeDtypeStruct((size, MEDIUM), jnp.bfloat16)
    wide_spec = pl.BlockSpec((MEDIUM, WIDTH), lambda i: (0, i))
    tall_spec = pl.BlockSpec((WIDTH, MEDIUM), lambda i: (i, 0))
    return pl.pallas_call(
        streams_kernel,
        out_shape=(wide, wide, tall, tall),
        grid=(size // WIDTH,),
        in_specs=[
            pl.BlockSpec((1, MEDIUM, WIDTH), lambda i: (0, 0, first + i)),
            pl.BlockSpec((RIM, WIDTH), lambda i: (0, first + i)),
            pl.BlockSpec((1, MEDIUM, WIDTH), lambda i: (0, 0, first + i)),
            pl.BlockSpec((1, MEDIUM), lambda i: (0, 0)),
            pl.BlockSpec((1, 3, SHORT, WIDTH), lambda i: (0, 0, 0, first + i)),
        ],
        out_specs=(wide_spec, wide_spec, tall_spec, tall_spec),
        name=f"streams_{start}",
    )(segment, rim, cotangent, domain, short_filters)


def input_grads(taps, mixed, before, grad, after, k, v, cotangent, domain, short_filters, start, size, base):
    first = start // WIDTH
    near = (start - base) // WIDTH
    groups = WIDTH // GSIZE
    wide_in = pl.BlockSpec((MEDIUM, WIDTH), lambda i: (0, near + i))
    tall_in = pl.BlockSpec((WIDTH, MEDIUM), lambda i: (near + i, 0))
    return pl.pallas_call(
        grads_kernel,
        out_shape=(
            jax.ShapeDtypeStruct((MEDIUM - RIM, size), jnp.bfloat16),
            jax.ShapeDtypeStruct((RIM, size), jnp.float32),
            jax.ShapeDtypeStruct((RIM, size), jnp.float32),
        ),
        grid=(size // WIDTH,),
        in_specs=[
            pl.BlockSpec((1, groups, MEDIUM), lambda i: (0, first + i, 0)),
            tall_in,
            tall_in,
            tall_in,
            tall_in,
            wide_in,
            wide_in,
            pl.BlockSpec((1, MEDIUM, WIDTH), lambda i: (0, 0, first + i)),
            pl.BlockSpec((1, MEDIUM), lambda i: (0, 0)),
            pl.BlockSpec((1, 3, SHORT, WIDTH), lambda i: (0, 0, 0, first + i)),
        ],
        out_specs=(
            pl.BlockSpec((MEDIUM - RIM, WIDTH), lambda i: (0, i)),
            pl.BlockSpec((RIM, WIDTH), lambda i: (0, i)),
            pl.BlockSpec((RIM, WIDTH), lambda i: (0, i)),
        ),
        scratch_shapes=[pltpu.VMEM((WIDTH, MEDIUM), jnp.bfloat16)] * 2,
        name=f"input_grads_{start}",
    )(taps, mixed, before, grad, after, k, v, cotangent, domain, short_filters)


def body(segment, cotangent, domain, short_filters, medium_filters):
    channels = segment.shape[2]
    ctx_count = lax.axis_size("ctx")
    pipe_count = lax.axis_size("pipe")
    onward, backward = ring_pairs(ctx_count, 1), ring_pairs(ctx_count, -1)
    passing = [(i, (i - 1) % pipe_count) for i in range(pipe_count)]
    unit = channels // 16

    rim = lax.ppermute(segment[0, MEDIUM - RIM :], "ctx", onward)
    halos, start = [], 0
    for part in HALO_PARTS:
        size = part * unit
        k, v, mixed, grad = streams(segment, rim, cotangent, domain, short_filters, start, size)
        before = lax.ppermute(mixed, "ctx", onward)
        after = lax.ppermute(grad, "ctx", backward)
        halos.append((start, size, (mixed, before, grad, after, k, v)))
        start += size
    passed, own, sent, start = [], [], [], 0
    for part in PASS_PARTS:
        size = part * unit
        base, _, arrays = next(h for h in halos if h[0] <= start < h[0] + h[1])
        out, own_part, sent_part = input_grads(
            medium_filters, *arrays, cotangent, domain, short_filters, start, size, base
        )
        passed.append((start, lax.ppermute(out, "pipe", passing)))
        own.append(own_part)
        sent.append(sent_part)
        start += size
    received = lax.ppermute(jnp.concatenate(sent, 1), "ctx", backward)
    last = (jnp.concatenate(own, 1) + received).astype(jnp.bfloat16)
    last = lax.ppermute(last, "pipe", passing)
    result = jnp.zeros((MEDIUM, channels), jnp.bfloat16)
    for start, out in passed:
        result = lax.dynamic_update_slice(result, out, (0, start))
    result = lax.dynamic_update_slice(result, last, (MEDIUM - RIM, 0))
    return result[None]


def solution(mesh):
    placed = (
        P("pipe", "ctx", None),
        P("pipe", "ctx", None),
        P("pipe", "ctx"),
        P("pipe", None, None, None),
        P("pipe", None, None),
    )
    return jax.shard_map(
        body, mesh=mesh, in_specs=placed, out_specs=P("pipe", "ctx", None), check_vma=False
    )
```

time: 357 us -> 111 us (0.31)
  local copies, waits for them, and re-layouts: 157 us -> 6.45 us
  other arithmetic: 74 us -> 0.79 us
  waiting for transfers between devices: 48.3 us -> 13.5 us
  Pallas kernels: 0 us -> 33.4 us
  blocking collectives: 20.9 us -> 0 us
    gather x4 -> x0, local copies, waits for them, and re-layouts: 123 us -> none  [the longest x2 61.4 us: toeplitz_pair(): far = jnp.take(filters, np.clip(lag_far, 0, MEDIUM - 1), axis=1)]
    convert_element_type x3 -> x1, other arithmetic: 54.5 us -> 0.02 us  [body(): last = (jnp.concatenate(own, 1) + received).astype(jnp.bfloat16)]
    pallas_call x0 -> x6, Pallas kernels: none -> 33.4 us  [the longest x4 20.1 us: input_grads(): pl.pallas_call(grads_kernel, out_shape=(jax.ShapeDtypeStruct((MEDIUM - RI...]
    ppermute x5 -> x11, starting transfers between devices: 23.4 us -> 54.4 us  [the longest x4 27.4 us: body(): passed.append((start, lax.ppermute(out, 'pipe', passing)))]
    all_to_all x3 -> x0, starting transfers between devices: 27.5 us -> none  [the longest x1 13.1 us: body(): lax.all_to_all(mixed, 'ctx', split_axis=1, concat_axis=0, tiled=True)]
    all_to_all x3 -> x0, waiting for transfers between devices: 23.4 us -> none  [the longest x1 13.4 us: body(): lax.all_to_all(out_ch, 'ctx', split_axis=0, concat_axis=1, tiled=True)]
    all_to_all x1 -> x0, blocking collectives: 20.9 us -> none  [body(): lax.all_to_all(conv_grad, 'ctx', split_axis=1, concat_axis=0, tiled=True)]
    mul x2 -> x0, other arithmetic: 18.5 us -> none  [the longest x1 16 us: body(): grad_query = gated * conv_out.astype(jnp.float32)]
  transfers between devices with their start and end apart: 8 -> 11, of which waited for: 4 -> 5; matrix products, arithmetic and copies ran while one was open for 39% -> 3% of each run, Pallas kernels for 0% -> 22%
where the time goes in v1:
time: 111 us; the launch traced here: 109 us
  starting transfers between devices  54.4 us (49%)
  Pallas kernels  33.4 us (30%)
  waiting for transfers between devices  13.5 us (12%)
  local copies, waits for them, and re-layouts  6.45 us (6%)
    ppermute x4, starting transfers between devices, body(): passed.append((start, lax.ppermute(out, 'pipe', passing)))  27.4 us
    pallas_call x4, Pallas kernels, input_grads(): pl.pallas_call(grads_kernel, out_shape=(jax.ShapeDtypeStruct((MEDIUM - RI...  20.1 us
    pallas_call x2, Pallas kernels, streams(): pl.pallas_call(streams_kernel, out_shape=(wide, wide, tall, tall), grid=(...  13.3 us
    ppermute x2, starting transfers between devices, body(): after = lax.ppermute(grad, 'ctx', backward)  11.5 us
    ppermute x1, starting transfers between devices, body(): received = lax.ppermute(jnp.concatenate(sent, 1), 'ctx', backward)  5.67 us
    ppermute x4, waiting for transfers between devices, body(): passed.append((start, lax.ppermute(out, 'pipe', passing)))  4.89 us
    unnamed x33, local copies, waits for them, and re-layouts  4.82 us
    ppermute x1, starting transfers between devices, body(): last = lax.ppermute(last, 'pipe', passing)  4.12 us
  transfers between devices with their start and end apart: 11, of which 5 were waited for; matrix products, arithmetic and copies ran while one was open for 3% of the time, Pallas kernels for 22%

profile of v1, /device:TPU:24, one launch (start us, length us, event | category | flops | bytes accessed | tf_op | source)
XLA Modules:
  0.0 108.9 jit_solution(4541266388733965816)
XLA Ops:
  0.0 0.8 slice_bitcast_fusion
  0.8 1.9 %collective-permute-start = (bf16[8,4096]{1,0:T(8,128)(2,1)S(1)}, bf16[8,4096]{1,0:T(8,128)(2,1)S(1)}, u32[]{:S(2)}, u32[]{:S(2)}) collective-permute-start(bf16[8,4096]{1,0:T(8,128)(2,1)S(1)} %slice_bitcast_fusion), channel_id=1, source_target_pairs={{0,1},{1,2},{2,3},{3,4},{4,5},{5,6},{6,7},{7,8},{8,9},{9,10},{10,1... | collective-permute-start | bytes 196616 | tf_op jit(solution)/shard_map/ppermute | solution.py:197
  2.8 2.0 %copy.6.short_ref = f32[1,3,7,4096]{3,2,1,0:T(8,128)} copy(f32[1,3,7,4096]{3,0,2,1:T(1,128)} %param.8) | data formatting | bytes 688128 | tf_op args[3]
  4.7 3.8 %collective-permute-done.rim_ref = bf16[8,4096]{1,0:T(8,128)(2,1)S(1)} collective-permute-done((bf16[8,4096]{1,0:T(8,128)(2,1)S(1)}, bf16[8,4096]{1,0:T(8,128)(2,1)S(1)}, u32[]{:S(2)}, u32[]{:S(2)}) %collective-permute-start) | collective-permute-done | bytes 65568 | tf_op jit(solution)/shard_map/ppermute | solution.py:197
  8.5 0.6 copy-done.3
  9.1 9.3 %streams_1024.1 = (bf16[128,3072]{1,0:T(8,128)(2,1)}, bf16[128,3072]{1,0:T(8,128)(2,1)}, bf16[3072,128]{1,0:T(8,128)(2,1)}, bf16[3072,128]{1,0:T(8,128)(2,1)}) custom-call(bf16[1,128,4096]{2,1,0:T(8,128)(2,1)} %seg_ref.3, bf16[8,4096]{1,0:T(8,128)(2,1)} %copy-done.3, bf16[1,128,4096]{2,1,0:T(8,128)(2,1)} %cot_ref.11, s32[1,128]{1,0:T(1,128)} %domain_ref.11, ...), custom_call_target="tpu_custom_call" | custom-call | tf_op jit(solution)/shard_map/streams_1024/pallas_call | solution.py:137
  18.5 1.9 %collective-permute-start.4 = (bf16[3072,128]{1,0:T(8,128)(2,1)}, bf16[3072,128]{1,0:T(8,128)(2,1)S(1)}, u32[]{:S(2)}, u32[]{:S(2)}) collective-permute-start(bf16[3072,128]{1,0:T(8,128)(2,1)} %get-tuple-element.30.mixed_ref), channel_id=1, source_target_pairs={{0,1},{1,2},{2,3},{3,4},{4,5},{5,6},{6,7},{7,8},{8,9},{9,10},{10,1... | collective-permute-start | bytes 2359304 | tf_op jit(solution)/shard_map/ppermute | solution.py:202
  20.4 5.8 %collective-permute-start.5 = (bf16[3072,128]{1,0:T(8,128)(2,1)}, bf16[3072,128]{1,0:T(8,128)(2,1)S(1)}, u32[]{:S(2)}, u32[]{:S(2)}) collective-permute-start(bf16[3072,128]{1,0:T(8,128)(2,1)} %get-tuple-element.31.grad_ref), channel_id=1, source_target_pairs={{1,0},{2,1},{3,2},{4,3},{5,4},{6,5},{7,6},{8,7},{9,8},{10,9},{11,1... | collective-permute-start | bytes 2359304 | tf_op jit(solution)/shard_map/ppermute | solution.py:203
  26.2 3.9 %streams_0.1 = (bf16[128,1024]{1,0:T(8,128)(2,1)}, bf16[128,1024]{1,0:T(8,128)(2,1)}, bf16[1024,128]{1,0:T(8,128)(2,1)}, bf16[1024,128]{1,0:T(8,128)(2,1)}) custom-call(bf16[1,128,4096]{2,1,0:T(8,128)(2,1)} %seg_ref.3, bf16[8,4096]{1,0:T(8,128)(2,1)} %copy-done.3, bf16[1,128,4096]{2,1,0:T(8,128)(2,1)} %cot_ref.11, s32[1,128]{1,0:T(1,128)} %domain_ref.11, ...), custom_call_target="tpu_custom_call" | custom-call | tf_op jit(solution)/shard_map/streams_0/pallas_call | solution.py:137
  30.1 1.9 %collective-permute-start.1 = (bf16[1024,128]{1,0:T(8,128)(2,1)}, bf16[1024,128]{1,0:T(8,128)(2,1)S(1)}, u32[]{:S(2)}, u32[]{:S(2)}) collective-permute-start(bf16[1024,128]{1,0:T(8,128)(2,1)} %get-tuple-element.25.mixed_ref), channel_id=1, source_target_pairs={{0,1},{1,2},{2,3},{3,4},{4,5},{5,6},{6,7},{7,8},{8,9},{9,10},{10,1... | collective-permute-start | bytes 786440 | tf_op jit(solution)/shard_map/ppermute | solution.py:202
  32.0 5.8 %collective-permute-start.2 = (bf16[1024,128]{1,0:T(8,128)(2,1)}, bf16[1024,128]{1,0:T(8,128)(2,1)S(1)}, u32[]{:S(2)}, u32[]{:S(2)}) collective-permute-start(bf16[1024,128]{1,0:T(8,128)(2,1)} %get-tuple-element.26.grad_ref), channel_id=1, source_target_pairs={{1,0},{2,1},{3,2},{4,3},{5,4},{6,5},{7,6},{8,7},{9,8},{10,9},{11,1... | collective-permute-start | bytes 786440 | tf_op jit(solution)/shard_map/ppermute | solution.py:203
  37.7 2.3 %collective-permute-done.1.before_ref = bf16[1024,128]{1,0:T(8,128)(2,1)S(1)} collective-permute-done((bf16[1024,128]{1,0:T(8,128)(2,1)}, bf16[1024,128]{1,0:T(8,128)(2,1)S(1)}, u32[]{:S(2)}, u32[]{:S(2)}) %collective-permute-start.1) | collective-permute-done | bytes 262176 | tf_op jit(solution)/shard_map/ppermute | solution.py:202
  40.1 1.9 %collective-permute-done.2.after_ref = bf16[1024,128]{1,0:T(8,128)(2,1)S(1)} collective-permute-done((bf16[1024,128]{1,0:T(8,128)(2,1)}, bf16[1024,128]{1,0:T(8,128)(2,1)S(1)}, u32[]{:S(2)}, u32[]{:S(2)}) %collective-permute-start.2) | collective-permute-done | bytes 262176 | tf_op jit(solution)/shard_map/ppermute | solution.py:203
  41.9 0.7 copy-done.5
  42.6 5.0 %input_grads_0.1 = (bf16[120,1024]{1,0:T(8,128)(2,1)}, f32[8,1024]{1,0:T(8,128)}, f32[8,1024]{1,0:T(8,128)}) custom-call(f32[1,256,128]{2,1,0:T(8,128)} %taps_ref.7, bf16[1024,128]{1,0:T(8,128)(2,1)} %get-tuple-element.25.mixed_ref, bf16[1024,128]{1,0:T(8,128)(2,1)} %copy-done.4, bf16[1024,128]{1,0:T(8,128)(2,1)} %get-tuple-element.26.grad_ref, ...), custom_call_target="tpu_custom_call" | custom-call | tf_op jit(solution)/shard_map/input_grads_0/pallas_call | solution.py:159
  47.7 18.7 %collective-permute-start.3 = (bf16[120,1024]{1,0:T(8,128)(2,1)}, bf16[120,1024]{1,0:T(8,128)(2,1)S(1)}, u32[]{:S(2)}, u32[]{:S(2)}) collective-permute-start(bf16[120,1024]{1,0:T(8,128)(2,1)} %get-tuple-element.29), channel_id=1, source_target_pairs={{0,992},{32,0},{64,32},{96,64},{128,96},{160,128},{192,160},{224,1... | collective-permute-start | bytes 737288 | tf_op jit(solution)/shard_map/ppermute | solution.py:213
  66.4 0.9 copy-done
  67.2 0.3 copy-done.1
  67.5 5.0 %input_grads_3072.1 = (bf16[120,1024]{1,0:T(8,128)(2,1)}, f32[8,1024]{1,0:T(8,128)}, f32[8,1024]{1,0:T(8,128)}) custom-call(f32[1,256,128]{2,1,0:T(8,128)} %taps_ref.7, bf16[3072,128]{1,0:T(8,128)(2,1)} %get-tuple-element.30.mixed_ref, bf16[3072,128]{1,0:T(8,128)(2,1)} %copy-done, bf16[3072,128]{1,0:T(8,128)(2,1)} %get-tuple-element.31.grad_ref, ...), custom_call_target="tpu_custom_call" | custom-call | tf_op jit(solution)/shard_map/input_grads_3072/pallas_call | solution.py:159
  72.6 5.0 %input_grads_2048.1 = (bf16[120,1024]{1,0:T(8,128)(2,1)}, f32[8,1024]{1,0:T(8,128)}, f32[8,1024]{1,0:T(8,128)}) custom-call(f32[1,256,128]{2,1,0:T(8,128)} %taps_ref.7, bf16[3072,128]{1,0:T(8,128)(2,1)} %get-tuple-element.30.mixed_ref, bf16[3072,128]{1,0:T(8,128)(2,1)} %copy-done, bf16[3072,128]{1,0:T(8,128)(2,1)} %get-tuple-element.31.grad_ref, ...), custom_call_target="tpu_custom_call" | custom-call | tf_op jit(solution)/shard_map/input_grads_2048/pallas_call | solution.py:159
  77.6 5.0 %input_grads_1024.1 = (bf16[120,1024]{1,0:T(8,128)(2,1)}, f32[8,1024]{1,0:T(8,128)}, f32[8,1024]{1,0:T(8,128)}) custom-call(f32[1,256,128]{2,1,0:T(8,128)} %taps_ref.7, bf16[3072,128]{1,0:T(8,128)(2,1)} %get-tuple-element.30.mixed_ref, bf16[3072,128]{1,0:T(8,128)(2,1)} %copy-done, bf16[3072,128]{1,0:T(8,128)(2,1)} %get-tuple-element.31.grad_ref, ...), custom_call_target="tpu_custom_call" | custom-call | tf_op jit(solution)/shard_map/input_grads_1024/pallas_call | solution.py:159
  82.7 0.8 pad_maximum_fusion
  83.5 5.7 %collective-permute-start.9 = (f32[8,4096]{1,0:T(8,128)S(1)}, f32[8,4096]{1,0:T(8,128)S(1)}, u32[]{:S(2)}, u32[]{:S(2)}) collective-permute-start(f32[8,4096]{1,0:T(8,128)S(1)} %pad_maximum_fusion), channel_id=1, source_target_pairs={{1,0},{2,1},{3,2},{4,3},{5,4},{6,5},{7,6},{8,7},{9,8},{10,9},{11,1... | collective-permute-start | bytes 393224 | tf_op jit(solution)/shard_map/ppermute | solution.py:217
  89.2 0.1 pad_bitcast_fusion
  89.3 2.9 %collective-permute-start.8 = (bf16[120,1024]{1,0:T(8,128)(2,1)S(1)}, bf16[120,1024]{1,0:T(8,128)(2,1)S(1)}, u32[]{:S(2)}, u32[]{:S(2)}) collective-permute-start(bf16[120,1024]{1,0:T(8,128)(2,1)S(1)} %copy-done.13), channel_id=1, source_target_pairs={{0,992},{32,0},{64,32},{96,64},{128,96},{160,128},{192,160},{224,1... | collective-permute-start | bytes 737288 | tf_op jit(solution)/shard_map/ppermute | solution.py:213
  92.3 2.9 %collective-permute-start.7 = (bf16[120,1024]{1,0:T(8,128)(2,1)S(1)}, bf16[120,1024]{1,0:T(8,128)(2,1)S(1)}, u32[]{:S(2)}, u32[]{:S(2)}) collective-permute-start(bf16[120,1024]{1,0:T(8,128)(2,1)S(1)} %copy-done.14), channel_id=1, source_target_pairs={{0,992},{32,0},{64,32},{96,64},{128,96},{160,128},{192,160},{224,1... | collective-permute-start | bytes 737288 | tf_op jit(solution)/shard_map/ppermute | solution.py:213
  95.2 2.9 %collective-permute-start.6 = (bf16[120,1024]{1,0:T(8,128)(2,1)S(1)}, bf16[120,1024]{1,0:T(8,128)(2,1)S(1)}, u32[]{:S(2)}, u32[]{:S(2)}) collective-permute-start(bf16[120,1024]{1,0:T(8,128)(2,1)S(1)} %copy-done.15), channel_id=1, source_target_pairs={{0,992},{32,0},{64,32},{96,64},{128,96},{160,128},{192,160},{224,1... | collective-permute-start | bytes 737288 | tf_op jit(solution)/shard_map/ppermute | solution.py:213
  98.2 4.1 %collective-permute-start.10 = (bf16[8,4096]{1,0:T(8,128)(2,1)S(1)}, bf16[8,4096]{1,0:T(8,128)(2,1)S(1)}, u32[]{:S(2)}, u32[]{:S(2)}) collective-permute-start(bf16[8,4096]{1,0:T(8,128)(2,1)S(1)} %fusion), channel_id=1, source_target_pairs={{0,992},{32,0},{64,32},{96,64},{128,96},{160,128},{192,160},{224,1... | collective-permute-start | bytes 196616 | tf_op jit(solution)/shard_map/ppermute | solution.py:219
  102.3 4.9 %collective-permute-done.6 = bf16[120,1024]{1,0:T(8,128)(2,1)S(1)} collective-permute-done((bf16[120,1024]{1,0:T(8,128)(2,1)S(1)}, bf16[120,1024]{1,0:T(8,128)(2,1)S(1)}, u32[]{:S(2)}, u32[]{:S(2)}) %collective-permute-start.6) | collective-permute-done | bytes 245792 | tf_op jit(solution)/shard_map/ppermute | solution.py:213
  107.3 0.6 collective-permute-done.10
  107.9 0.4 copy-done.2
  108.3 0.6 bitcast_dynamic-update-slice_fusion.3
  (37 shorter events, 0.1 us)
Async XLA Ops:
  0.8 7.7 %collective-permute-start = (bf16[8,4096]{1,0:T(8,128)(2,1)S(1)}, bf16[8,4096]{1,0:T(8,128)(2,1)S(1)}, u32[]{:S(2)}, u32[]{:S(2)}) collective-permute-start(bf16[8,4096]{1,0:T(8,128)(2,1)S(1)} %slice_bitcast_fusion), channel_id=1, source_target_pairs={{0,1},{1,2},{2,3},{3,4},{4,5},{5,6},{6,7},{7,8},{8,9},{9,10},{10,1... | collective-permute-start | bytes 196616 | tf_op jit(solution)/shard_map/ppermute | solution.py:197
  8.5 0.6 copy-start.3
  18.5 47.9 %collective-permute-start.4 = (bf16[3072,128]{1,0:T(8,128)(2,1)}, bf16[3072,128]{1,0:T(8,128)(2,1)S(1)}, u32[]{:S(2)}, u32[]{:S(2)}) collective-permute-start(bf16[3072,128]{1,0:T(8,128)(2,1)} %get-tuple-element.30.mixed_ref), channel_id=1, source_target_pairs={{0,1},{1,2},{2,3},{3,4},{4,5},{5,6},{6,7},{7,8},{8,9},{9,10},{10,1... | collective-permute-start | bytes 2359304 | tf_op jit(solution)/shard_map/ppermute | solution.py:202
  20.4 46.0 %collective-permute-start.5 = (bf16[3072,128]{1,0:T(8,128)(2,1)}, bf16[3072,128]{1,0:T(8,128)(2,1)S(1)}, u32[]{:S(2)}, u32[]{:S(2)}) collective-permute-start(bf16[3072,128]{1,0:T(8,128)(2,1)} %get-tuple-element.31.grad_ref), channel_id=1, source_target_pairs={{1,0},{2,1},{3,2},{4,3},{5,4},{6,5},{7,6},{8,7},{9,8},{10,9},{11,1... | collective-permute-start | bytes 2359304 | tf_op jit(solution)/shard_map/ppermute | solution.py:203
  30.1 10.0 %collective-permute-start.1 = (bf16[1024,128]{1,0:T(8,128)(2,1)}, bf16[1024,128]{1,0:T(8,128)(2,1)S(1)}, u32[]{:S(2)}, u32[]{:S(2)}) collective-permute-start(bf16[1024,128]{1,0:T(8,128)(2,1)} %get-tuple-element.25.mixed_ref), channel_id=1, source_target_pairs={{0,1},{1,2},{2,3},{3,4},{4,5},{5,6},{6,7},{7,8},{8,9},{9,10},{10,1... | collective-permute-start | bytes 786440 | tf_op jit(solution)/shard_map/ppermute | solution.py:202
  32.0 9.9 %collective-permute-start.2 = (bf16[1024,128]{1,0:T(8,128)(2,1)}, bf16[1024,128]{1,0:T(8,128)(2,1)S(1)}, u32[]{:S(2)}, u32[]{:S(2)}) collective-permute-start(bf16[1024,128]{1,0:T(8,128)(2,1)} %get-tuple-element.26.grad_ref), channel_id=1, source_target_pairs={{1,0},{2,1},{3,2},{4,3},{5,4},{6,5},{7,6},{8,7},{9,8},{10,9},{11,1... | collective-permute-start | bytes 786440 | tf_op jit(solution)/shard_map/ppermute | solution.py:203
  40.1 1.9 %copy-start.4 = (bf16[1024,128]{1,0:T(8,128)(2,1)}, bf16[1024,128]{1,0:T(8,128)(2,1)S(1)}, u32[]{:S(2)}) copy-start(bf16[1024,128]{1,0:T(8,128)(2,1)S(1)} %collective-permute-done.1.before_ref) | copy-start | bytes 786436
  41.9 0.7 copy-start.5
  47.7 41.5 %collective-permute-start.3 = (bf16[120,1024]{1,0:T(8,128)(2,1)}, bf16[120,1024]{1,0:T(8,128)(2,1)S(1)}, u32[]{:S(2)}, u32[]{:S(2)}) collective-permute-start(bf16[120,1024]{1,0:T(8,128)(2,1)} %get-tuple-element.29), channel_id=1, source_target_pairs={{0,992},{32,0},{64,32},{96,64},{128,96},{160,128},{192,160},{224,1... | collective-permute-start | bytes 737288 | tf_op jit(solution)/shard_map/ppermute | solution.py:213
  66.4 0.9 copy-start
  66.4 1.2 %copy-start.1 = (bf16[3072,128]{1,0:T(8,128)(2,1)}, bf16[3072,128]{1,0:T(8,128)(2,1)S(1)}, u32[]{:S(2)}) copy-start(bf16[3072,128]{1,0:T(8,128)(2,1)S(1)} %collective-permute-done.5.after_ref) | copy-start | bytes 2359300
  77.6 5.1 %copy-start.10 = (f32[8,1024]{1,0:T(8,128)S(1)}, f32[8,1024]{1,0:T(8,128)}, u32[]{:S(2)}) copy-start(f32[8,1024]{1,0:T(8,128)} %get-tuple-element.41) | copy-start | bytes 98308
  77.6 5.1 %copy-start.11 = (f32[8,1024]{1,0:T(8,128)S(1)}, f32[8,1024]{1,0:T(8,128)}, u32[]{:S(2)}) copy-start(f32[8,1024]{1,0:T(8,128)} %get-tuple-element.44) | copy-start | bytes 98308
  77.6 5.1 %copy-start.12 = (f32[8,1024]{1,0:T(8,128)S(1)}, f32[8,1024]{1,0:T(8,128)}, u32[]{:S(2)}) copy-start(f32[8,1024]{1,0:T(8,128)} %get-tuple-element.43) | copy-start | bytes 98308
  83.5 5.9 %copy-start.13 = (bf16[120,1024]{1,0:T(8,128)(2,1)S(1)}, bf16[120,1024]{1,0:T(8,128)(2,1)}, u32[]{:S(2)}) copy-start(bf16[120,1024]{1,0:T(8,128)(2,1)} %get-tuple-element.36) | copy-start | bytes 737284
  83.5 8.8 %copy-start.14 = (bf16[120,1024]{1,0:T(8,128)(2,1)S(1)}, bf16[120,1024]{1,0:T(8,128)(2,1)}, u32[]{:S(2)}) copy-start(bf16[120,1024]{1,0:T(8,128)(2,1)} %get-tuple-element.35) | copy-start | bytes 737284
  83.5 11.7 %copy-start.15 = (bf16[120,1024]{1,0:T(8,128)(2,1)S(1)}, bf16[120,1024]{1,0:T(8,128)(2,1)}, u32[]{:S(2)}) copy-start(bf16[120,1024]{1,0:T(8,128)(2,1)} %get-tuple-element.34) | copy-start | bytes 737284
  83.5 14.6 %collective-permute-start.9 = (f32[8,4096]{1,0:T(8,128)S(1)}, f32[8,4096]{1,0:T(8,128)S(1)}, u32[]{:S(2)}, u32[]{:S(2)}) collective-permute-start(f32[8,4096]{1,0:T(8,128)S(1)} %pad_maximum_fusion), channel_id=1, source_target_pairs={{1,0},{2,1},{3,2},{4,3},{5,4},{6,5},{7,6},{8,7},{9,8},{10,9},{11,1... | collective-permute-start | bytes 393224 | tf_op jit(solution)/shard_map/ppermute | solution.py:217
  89.2 9.0 %copy-start.6 = (f32[8,1024]{1,0:T(8,128)S(1)}, f32[8,1024]{1,0:T(8,128)}, u32[]{:S(2)}) copy-start(f32[8,1024]{1,0:T(8,128)} %get-tuple-element.37) | copy-start | bytes 98308
  89.2 9.0 %copy-start.7 = (f32[8,1024]{1,0:T(8,128)S(1)}, f32[8,1024]{1,0:T(8,128)}, u32[]{:S(2)}) copy-start(f32[8,1024]{1,0:T(8,128)} %get-tuple-element.40) | copy-start | bytes 98308
  89.2 9.0 %copy-start.8 = (f32[8,1024]{1,0:T(8,128)S(1)}, f32[8,1024]{1,0:T(8,128)}, u32[]{:S(2)}) copy-start(f32[8,1024]{1,0:T(8,128)} %get-tuple-element.39) | copy-start | bytes 98308
  89.2 9.0 %copy-start.9 = (f32[8,1024]{1,0:T(8,128)S(1)}, f32[8,1024]{1,0:T(8,128)}, u32[]{:S(2)}) copy-start(f32[8,1024]{1,0:T(8,128)} %get-tuple-element.38) | copy-start | bytes 98308
  89.3 17.9 %collective-permute-start.8 = (bf16[120,1024]{1,0:T(8,128)(2,1)S(1)}, bf16[120,1024]{1,0:T(8,128)(2,1)S(1)}, u32[]{:S(2)}, u32[]{:S(2)}) collective-permute-start(bf16[120,1024]{1,0:T(8,128)(2,1)S(1)} %copy-done.13), channel_id=1, source_target_pairs={{0,992},{32,0},{64,32},{96,64},{128,96},{160,128},{192,160},{224,1... | collective-permute-start | bytes 737288 | tf_op jit(solution)/shard_map/ppermute | solution.py:213
  92.3 15.0 %collective-permute-start.7 = (bf16[120,1024]{1,0:T(8,128)(2,1)S(1)}, bf16[120,1024]{1,0:T(8,128)(2,1)S(1)}, u32[]{:S(2)}, u32[]{:S(2)}) collective-permute-start(bf16[120,1024]{1,0:T(8,128)(2,1)S(1)} %copy-done.14), channel_id=1, source_target_pairs={{0,992},{32,0},{64,32},{96,64},{128,96},{160,128},{192,160},{224,1... | collective-permute-start | bytes 737288 | tf_op jit(solution)/shard_map/ppermute | solution.py:213
  95.2 12.0 %collective-permute-start.6 = (bf16[120,1024]{1,0:T(8,128)(2,1)S(1)}, bf16[120,1024]{1,0:T(8,128)(2,1)S(1)}, u32[]{:S(2)}, u32[]{:S(2)}) collective-permute-start(bf16[120,1024]{1,0:T(8,128)(2,1)S(1)} %copy-done.15), channel_id=1, source_target_pairs={{0,992},{32,0},{64,32},{96,64},{128,96},{160,128},{192,160},{224,1... | collective-permute-start | bytes 737288 | tf_op jit(solution)/shard_map/ppermute | solution.py:213
  98.2 9.7 %collective-permute-start.10 = (bf16[8,4096]{1,0:T(8,128)(2,1)S(1)}, bf16[8,4096]{1,0:T(8,128)(2,1)S(1)}, u32[]{:S(2)}, u32[]{:S(2)}) collective-permute-start(bf16[8,4096]{1,0:T(8,128)(2,1)S(1)} %fusion), channel_id=1, source_target_pairs={{0,992},{32,0},{64,32},{96,64},{128,96},{160,128},{192,160},{224,1... | collective-permute-start | bytes 196616 | tf_op jit(solution)/shard_map/ppermute | solution.py:219
  107.3 1.0 copy-start.2

commit v2 on v1

v2 whole, which is shorter than its diff:
```python
import jax
import jax.numpy as jnp
from jax import lax
from jax.experimental import pallas as pl
from jax.experimental.pallas import tpu as pltpu
from jax.sharding import PartitionSpec as P


SHORT = 7
MEDIUM = 128
GSIZE = 16
LANES = 128
RIM = 8
WIDTH = 512
ROWS = 32

loss_table = [0.5, 1.0, 1.5, 2.0, 3.0, 0.25, 1.25, 2.5]

HALO_PARTS = (8, 8)
PASS_PARTS = (4, 4, 4, 4)

whole = pl.BlockSpec(memory_space=pltpu.VMEM)


def in_vmem(x):
    return pltpu.with_memory_space_constraint(x, pltpu.VMEM)


def in_hbm(x):
    return pltpu.with_memory_space_constraint(x, pltpu.HBM)


def token_weights(domain_ref):
    ids = domain_ref[...]
    row = jnp.zeros(ids.shape, jnp.float32)
    for index, value in enumerate(loss_table):
        row = jnp.where(ids == index, jnp.float32(value), row)
    return jnp.broadcast_to(row, (MEDIUM, MEDIUM)).T


def square(test):
    rows = lax.broadcasted_iota(jnp.int32, (MEDIUM, MEDIUM), 0)
    cols = lax.broadcasted_iota(jnp.int32, (MEDIUM, MEDIUM), 1)
    return test(rows, cols).astype(jnp.float32).astype(jnp.bfloat16)


def reversal():
    return square(lambda r, c: r + c == MEDIUM - 1)


def identity():
    return square(lambda r, c: r == c)


def streams_kernel(
    parity_ref, seg_ref, rim_ref, cot_ref, domain_ref, short_ref, after_ref,
    k_ref, v_ref, first_ref, second_ref, token_ref, weight_ref, x_ref, mixed_ref, grad_ref, *, start,
):
    step = pl.program_id(0)
    even = parity_ref[0] == 0

    @pl.when(step == 0)
    def _():
        weight_ref[...] = token_weights(domain_ref)
        token_ref[...] = jnp.zeros_like(token_ref)

    flip = reversal()
    for b in range(seg_ref.shape[2] // LANES):
        cols = pl.ds(b * LANES, LANES)
        x_ref[b, :RIM, :] = rim_ref[:, pl.ds(pl.multiple_of(start + step * WIDTH + b * LANES, LANES), LANES)].astype(jnp.float32)
        x_ref[b, RIM:, :] = seg_ref[0, :, cols].astype(jnp.float32)
        out_cols = pl.ds(pl.multiple_of(step * WIDTH + b * LANES, LANES), LANES)
        taps = [[short_ref[i * SHORT + j, :, cols] for j in range(SHORT)] for i in range(3)]
        for r in range(0, MEDIUM, ROWS):
            sums = [None, None, None]
            for j in range(SHORT):
                moved = x_ref[b, pl.ds(RIM + r - j, ROWS), :]
                for i in range(3):
                    term = taps[i][j] * moved
                    sums[i] = term if j == 0 else sums[i] + term
            q, k, v = sums
            rows = pl.ds(r, ROWS)
            k_ref[rows, out_cols] = k.astype(jnp.bfloat16)
            v_ref[rows, out_cols] = v.astype(jnp.bfloat16)
            mixed_ref[b, rows, :] = k * v
            gated = cot_ref[0, rows, cols].astype(jnp.float32) * weight_ref[rows, :]
            grad_ref[b, rows, :] = (q * gated).astype(jnp.bfloat16)
        mixed = mixed_ref[b].T.astype(jnp.bfloat16)
        back = jnp.dot(flip, grad_ref[b], preferred_element_type=jnp.float32)
        grad = back.T.astype(jnp.bfloat16)
        out_rows = pl.ds(pl.multiple_of(step * WIDTH + b * LANES, LANES), LANES)
        first_ref[out_rows, :] = jnp.where(even, mixed, grad)
        second_ref[out_rows, :] = jnp.where(even, grad, mixed)


def toeplitz_kernel(taps_ref, matrix_ref):
    step = pl.program_id(0)
    near_mask = square(lambda r, c: c >= r)
    far_mask = square(lambda r, c: c < r)
    groups = taps_ref.shape[1]
    for g in range(groups):
        taps = taps_ref[0, pl.ds(g, 1), :].astype(jnp.bfloat16).astype(jnp.float32)
        spread = jnp.broadcast_to(taps, (MEDIUM, MEDIUM))
        circle = pltpu.roll(spread, 0, 1, stride=1, stride_axis=0).astype(jnp.bfloat16)
        matrix_ref[step * groups + g, :MEDIUM, :] = circle * far_mask
        matrix_ref[step * groups + g, MEDIUM:, :] = circle * near_mask


def grads_kernel(
    parity_ref, matrix_ref, first_ref, first_got_ref, second_ref, second_got_ref, k_ref, v_ref,
    cot_ref, domain_ref, short_ref, after_ref,
    out_ref, own_ref, sent_ref, weight_ref, part_ref, *, start, base,
):
    step = pl.program_id(0)
    even = parity_ref[0] == 0
    width = cot_ref.shape[2]
    blocks = width // LANES
    per_block = LANES // GSIZE

    @pl.when(step == 0)
    def _():
        weight_ref[...] = token_weights(domain_ref)
        blank = jnp.zeros((RIM, LANES), jnp.float32)
        for b in range(blocks):
            for j in range(SHORT):
                part_ref[b, j, :RIM, :] = blank
                part_ref[b, j, RIM + MEDIUM :, :] = blank

    keep, flip = identity(), reversal()
    contract = (((1,), (1,)), ((), ()))
    here = pl.multiple_of(start - base + step * width, width)
    first_group = start // GSIZE + step * (width // GSIZE)

    def products(b):
        convs, backs = [], []
        for g in range(per_block):
            at = pl.ds(pl.multiple_of(here + b * LANES + g * GSIZE, GSIZE), GSIZE)
            windows = jnp.concatenate(
                [
                    jnp.concatenate([second_got_ref[at, :], first_ref[at, :]], 1),
                    jnp.concatenate([first_got_ref[at, :], second_ref[at, :]], 1),
                ],
                0,
            )
            matrix = matrix_ref[first_group + b * per_block + g]
            both = jnp.dot(windows, matrix, preferred_element_type=jnp.float32).astype(jnp.bfloat16)
            convs.append(jnp.where(even, both[:GSIZE], both[GSIZE:]))
            backs.append(jnp.where(even, both[GSIZE:], both[:GSIZE]))
        return jnp.concatenate(convs, 0), jnp.concatenate(backs, 0)

    coming = products(0)
    for b in range(blocks):
        conv_rows, back_rows = coming
        if b + 1 < blocks:
            coming = products(b + 1)
        at = pl.ds(b * LANES, LANES)
        in_cols = pl.ds(pl.multiple_of(here + b * LANES, LANES), LANES)
        out_cols = pl.ds(pl.multiple_of(step * width + b * LANES, LANES), LANES)
        conv = lax.dot_general(keep, conv_rows, contract, preferred_element_type=jnp.float32)
        back = lax.dot_general(flip, back_rows, contract, preferred_element_type=jnp.float32)
        taps = [[short_ref[i * SHORT + j, :, at] for j in range(SHORT)] for i in range(3)]
        for r in range(0, MEDIUM, ROWS):
            rows = pl.ds(r, ROWS)
            gated = cot_ref[0, rows, at].astype(jnp.float32) * weight_ref[rows, :]
            lag = back[r : r + ROWS]
            grads = (
                gated * conv[r : r + ROWS],
                lag * v_ref[rows, in_cols].astype(jnp.float32),
                lag * k_ref[rows, in_cols].astype(jnp.float32),
            )
            for j in range(SHORT):
                part = taps[0][j] * grads[0] + taps[1][j] * grads[1] + taps[2][j] * grads[2]
                part_ref[b, j, pl.ds(RIM + r, ROWS), :] = part
        sent = part_ref[b, 1, pl.ds(1, RIM), :]
        for j in range(2, SHORT):
            sent = sent + part_ref[b, j, pl.ds(j, RIM), :]
        sent_ref[:, out_cols] = sent
        for r in range(0, MEDIUM, ROWS):
            total = part_ref[b, 0, pl.ds(RIM + r, ROWS), :]
            for j in range(1, SHORT):
                total = total + part_ref[b, j, pl.ds(RIM + r + j, ROWS), :]
            if r + ROWS < MEDIUM:
                out_ref[pl.ds(r, ROWS), out_cols] = total.astype(jnp.bfloat16)
            else:
                out_ref[pl.ds(r, ROWS - RIM), out_cols] = total[: ROWS - RIM].astype(jnp.bfloat16)
                own_ref[:, out_cols] = total[ROWS - RIM :]


def toeplitz(taps):
    _, groups, count = taps.shape
    return pl.pallas_call(
        toeplitz_kernel,
        out_shape=pltpu.VMEM((groups, 2 * count, count), jnp.bfloat16),
        grid=(groups // GSIZE,),
        in_specs=[pl.BlockSpec((1, GSIZE, count), lambda i: (0, i, 0))],
        out_specs=whole,
        compiler_params=pltpu.CompilerParams(vmem_limit_bytes=24 << 20),
        name="toeplitz",
    )(taps)


def streams(parity, segment, rim, cotangent, domain, short, after, start, size):
    first = start // WIDTH
    wide = pltpu.VMEM((MEDIUM, size), jnp.bfloat16)
    tall = pltpu.VMEM((size, MEDIUM), jnp.bfloat16)
    blocks = WIDTH // LANES

    def kernel(*refs):
        streams_kernel(*refs, start=start)

    return pl.pallas_call(
        kernel,
        out_shape=(wide, wide, tall, tall, pltpu.VMEM((RIM, LANES), jnp.float32)),
        grid=(size // WIDTH,),
        in_specs=[
            pl.BlockSpec(memory_space=pltpu.SMEM),
            pl.BlockSpec((1, MEDIUM, WIDTH), lambda i: (0, 0, first + i)),
            whole,
            pl.BlockSpec((1, MEDIUM, WIDTH), lambda i: (0, 0, first + i)),
            pl.BlockSpec((1, MEDIUM), lambda i: (0, 0)),
            pl.BlockSpec((3 * SHORT, 1, WIDTH), lambda i: (0, 0, first + i)),
            whole,
        ],
        out_specs=(whole,) * 5,
        scratch_shapes=[
            pltpu.VMEM((MEDIUM, LANES), jnp.float32),
            pltpu.VMEM((blocks, RIM + MEDIUM, LANES), jnp.float32),
            pltpu.VMEM((blocks, MEDIUM, LANES), jnp.float32),
            pltpu.VMEM((blocks, MEDIUM, LANES), jnp.bfloat16),
        ],
        compiler_params=pltpu.CompilerParams(vmem_limit_bytes=24 << 20),
    )(parity, segment, rim, cotangent, domain, short, after)


def input_grads(parity, matrices, arrays, cotangent, domain, short, after, start, size, base):
    first = start // WIDTH
    blocks = WIDTH // LANES

    def kernel(*refs):
        grads_kernel(*refs, start=start, base=base)

    return pl.pallas_call(
        kernel,
        out_shape=(
            pltpu.VMEM((MEDIUM - RIM, size), jnp.bfloat16),
            pltpu.VMEM((RIM, size), jnp.float32),
            pltpu.VMEM((RIM, size), jnp.float32),
        ),
        grid=(size // WIDTH,),
        in_specs=[
            pl.BlockSpec(memory_space=pltpu.SMEM),
            whole,
            whole,
            whole,
            whole,
            whole,
            whole,
            whole,
            pl.BlockSpec((1, MEDIUM, WIDTH), lambda i: (0, 0, first + i)),
            pl.BlockSpec((1, MEDIUM), lambda i: (0, 0)),
            pl.BlockSpec((3 * SHORT, 1, WIDTH), lambda i: (0, 0, first + i)),
            whole,
        ],
        out_specs=(whole,) * 3,
        scratch_shapes=[
            pltpu.VMEM((MEDIUM, LANES), jnp.float32),
            pltpu.VMEM((blocks, SHORT, MEDIUM + 2 * RIM, LANES), jnp.float32),
        ],
        compiler_params=pltpu.CompilerParams(vmem_limit_bytes=24 << 20),
    )(parity, matrices, *arrays, cotangent, domain, short, after)


def exchange_pairs(count, odd):
    pairs = []
    for low in range(odd, count - 1, 2):
        pairs += [(low, low + 1), (low + 1, low)]
    return pairs


def body(segment, cotangent, domain, short_filters, medium_filters):
    channels = segment.shape[2]
    ctx_count = lax.axis_size("ctx")
    pipe_count = lax.axis_size("pipe")
    onward = [(i, i + 1) for i in range(ctx_count - 1)]
    backward = [(i + 1, i) for i in range(ctx_count - 1)]
    inner, outer = exchange_pairs(ctx_count, 0), exchange_pairs(ctx_count, 1)
    passing = [(i, (i - 1) % pipe_count) for i in range(pipe_count)]
    unit = channels // 16
    parity = jnp.full((1,), lax.axis_index("ctx") % 2, jnp.int32)
    short = jnp.transpose(short_filters, (1, 2, 0, 3)).reshape(3 * SHORT, 1, channels)

    rim = in_vmem(lax.ppermute(segment[0, MEDIUM - RIM :], "ctx", onward))
    segment, cotangent, short, domain, medium_filters = map(
        in_hbm, (segment, cotangent, short, domain, medium_filters)
    )
    matrices = in_vmem(toeplitz(medium_filters))
    halos, start, after = [], 0, rim
    for part in HALO_PARTS:
        size = part * unit
        results = streams(parity, segment, rim, cotangent, domain, short, after, start, size)
        k, v, first, second, after = map(in_vmem, results)
        first_got = in_vmem(lax.ppermute(first, "ctx", inner))
        second_got = in_vmem(lax.ppermute(second, "ctx", outer))
        halos.append((start, size, (first, first_got, second, second_got, k, v)))
        start += size
    passed, own, sent, start = [], [], [], 0
    for part in PASS_PARTS:
        size = part * unit
        base, _, arrays = next(h for h in halos if h[0] <= start < h[0] + h[1])
        out, own_part, sent_part = input_grads(
            parity, matrices, arrays, cotangent, domain, short, after, start, size, base
        )
        passed.append((start, lax.ppermute(out, "pipe", passing)))
        own.append(own_part)
        sent.append(sent_part)
        start += size
        after = in_vmem(own_part)
    received = lax.ppermute(jnp.concatenate(sent, 1), "ctx", backward)
    last = (jnp.concatenate(own, 1) + received).astype(jnp.bfloat16)
    last = lax.ppermute(last, "pipe", passing)
    result = jnp.zeros((MEDIUM, channels), jnp.bfloat16)
    for start, out in passed:
        result = lax.dynamic_update_slice(result, out, (0, start))
    result = lax.dynamic_update_slice(result, last, (MEDIUM - RIM, 0))
    return result[None]


def solution(mesh):
    placed = (
        P("pipe", "ctx", None),
        P("pipe", "ctx", None),
        P("pipe", "ctx"),
        P("pipe", None, None, None),
        P("pipe", None, None),
    )

    return jax.shard_map(
        body, mesh=mesh, in_specs=placed, out_specs=P("pipe", "ctx", None), check_vma=False
    )
```

time: 111 us -> 94.1 us (0.85)
  starting transfers between devices: 54.4 us -> 47.8 us
  Pallas kernels: 33.4 us -> 28.1 us
  local copies, waits for them, and re-layouts: 6.45 us -> 2.12 us
  waiting for transfers between devices: 13.5 us -> 14.8 us
    pallas_call x6 -> x7, Pallas kernels: 33.4 us -> 28.1 us  [the longest x4 12.4 us: input_grads(): pl.pallas_call(kernel, out_shape=(pltpu.VMEM((MEDIUM - RIM, size), jnp.bf...]
    unnamed x33 -> x2, local copies, waits for them, and re-layouts: 4.82 us -> 0.49 us
    ppermute x5, starting transfers between devices: 17.2 us -> 13.4 us  [the longest x2 7.67 us: body(): second_got = in_vmem(lax.ppermute(second, 'ctx', outer))]
    ppermute x4, waiting for transfers between devices: 4.89 us -> 8.51 us  [body(): passed.append((start, lax.ppermute(out, 'pipe', passing)))]
    ppermute x1, starting transfers between devices: 5.67 us -> 2.84 us  [body(): received = lax.ppermute(jnp.concatenate(sent, 1), 'ctx', backward)]
    ppermute x5, waiting for transfers between devices: 8 us -> 5.77 us  [the longest x1 5.76 us: body(): rim = in_vmem(lax.ppermute(segment[0, MEDIUM - RIM:], 'ctx', onward))]
  transfers between devices with their start and end apart: 11 -> 11, of which waited for: 5 -> 3; matrix products, arithmetic and copies ran while one was open for 3% -> 0% of each run, Pallas kernels for 22% -> 19%
where the time goes in v2:
time: 94.1 us; the launch traced here: 93.1 us
  starting transfers between devices  47.8 us (51%)
  Pallas kernels  28.1 us (30%)
  waiting for transfers between devices  14.8 us (16%)
  local copies, waits for them, and re-layouts  2.12 us (2%)
    ppermute x4, starting transfers between devices, body(): passed.append((start, lax.ppermute(out, 'pipe', passing)))  27.4 us
    pallas_call x4, Pallas kernels, input_grads(): pl.pallas_call(kernel, out_shape=(pltpu.VMEM((MEDIUM - RIM, size), jnp.bf...  12.4 us
    ppermute x4, waiting for transfers between devices, body(): passed.append((start, lax.ppermute(out, 'pipe', passing)))  8.51 us
    pallas_call x2, Pallas kernels, streams(): pl.pallas_call(kernel, out_shape=(wide, wide, tall, tall, pltpu.VMEM((RIM...  7.89 us
    pallas_call x1, Pallas kernels, toeplitz(): pl.pallas_call(toeplitz_kernel, out_shape=pltpu.VMEM((groups, 2 * count,...  7.78 us
    ppermute x2, starting transfers between devices, body(): second_got = in_vmem(lax.ppermute(second, 'ctx', outer))  7.67 us
    ppermute x1, waiting for transfers between devices, body(): rim = in_vmem(lax.ppermute(segment[0, MEDIUM - RIM:], 'ctx', onward))  5.76 us
    ppermute x1, starting transfers between devices, body(): last = lax.ppermute(last, 'pipe', passing)  4.12 us
  transfers between devices with their start and end apart: 11, of which 3 were waited for; matrix products, arithmetic and copies ran while one was open for 0% of the time, Pallas kernels for 19%

profile of v2, /device:TPU:24, one launch (start us, length us, event | category | flops | bytes accessed | tf_op | source)
XLA Modules:
  0.0 93.1 jit_solution(18149462727890384891)
XLA Ops:
  0.0 0.8 slice_bitcast_fusion
  0.8 1.9 %collective-permute-start = (bf16[8,4096]{1,0:T(8,128)(2,1)S(1)}, bf16[8,4096]{1,0:T(8,128)(2,1)S(1)}, u32[]{:S(2)}, u32[]{:S(2)}) collective-permute-start(bf16[8,4096]{1,0:T(8,128)(2,1)S(1)} %slice_bitcast_fusion), channel_id=1, source_target_pairs={{0,1},{1,2},{2,3},{3,4},{4,5},{5,6},{6,7},{7,8},{8,9},{9,10},{10,1... | collective-permute-start | bytes 196616 | tf_op jit(solution)/shard_map/ppermute | solution.py:292
  2.8 5.8 %collective-permute-done.refs_2_.refs_6_ = bf16[8,4096]{1,0:T(8,128)(2,1)S(1)} collective-permute-done((bf16[8,4096]{1,0:T(8,128)(2,1)S(1)}, bf16[8,4096]{1,0:T(8,128)(2,1)S(1)}, u32[]{:S(2)}, u32[]{:S(2)}) %collective-permute-start) | collective-permute-done | bytes 65568 | tf_op jit(solution)/shard_map/ppermute | solution.py:292
  8.5 3.9 %shard_map.55 = (bf16[128,2048]{1,0:T(8,128)(2,1)S(1)}, bf16[128,2048]{1,0:T(8,128)(2,1)S(1)}, bf16[2048,128]{1,0:T(8,128)(2,1)S(1)}, bf16[2048,128]{1,0:T(8,128)(2,1)S(1)}, f32[8,128]{1,0:T(8,128)S(1)}) custom-call(s32[1]{0:T(128)} %bitcast.refs_0_, bf16[1,128,4096]{2,1,0:T(8,128)(2,1)} %refs_1_.3, ...), custom_call_target="tpu_custom_call" | custom-call | tf_op jit(solution)/shard_map/pallas_call | solution.py:211
  12.4 1.9 %collective-permute-start.1 = (bf16[2048,128]{1,0:T(8,128)(2,1)S(1)}, bf16[2048,128]{1,0:T(8,128)(2,1)S(1)}, u32[]{:S(2)}, u32[]{:S(2)}) collective-permute-start(bf16[2048,128]{1,0:T(8,128)(2,1)S(1)} %get-tuple-element.27.refs_2_), channel_id=1, source_target_pairs={{0,1},{1,0},{2,3},{3,2},{4,5},{5,4},{6,7},{7,6},{8,9},{9,8},{10,11... | collective-permute-start | bytes 1572872 | tf_op jit(solution)/shard_map/ppermute | solution.py:302
  14.4 2.8 %collective-permute-start.2 = (bf16[2048,128]{1,0:T(8,128)(2,1)S(1)}, bf16[2048,128]{1,0:T(8,128)(2,1)S(1)}, u32[]{:S(2)}, u32[]{:S(2)}) collective-permute-start(bf16[2048,128]{1,0:T(8,128)(2,1)S(1)} %get-tuple-element.28.refs_4_), channel_id=1, source_target_pairs={{1,2},{2,1},{3,4},{4,3},{5,6},{6,5},{7,8},{8,7},{9,10},{10,9},{11,... | collective-permute-start | bytes 1572872 | tf_op jit(solution)/shard_map/ppermute | solution.py:303
  17.2 4.0 %shard_map.56 = (bf16[128,2048]{1,0:T(8,128)(2,1)S(1)}, bf16[128,2048]{1,0:T(8,128)(2,1)S(1)}, bf16[2048,128]{1,0:T(8,128)(2,1)S(1)}, bf16[2048,128]{1,0:T(8,128)(2,1)S(1)}, f32[8,128]{1,0:T(8,128)S(1)}) custom-call(s32[1]{0:T(128)} %bitcast.refs_0_, bf16[1,128,4096]{2,1,0:T(8,128)(2,1)} %refs_1_.3, ...), custom_call_target="tpu_custom_call" | custom-call | tf_op jit(solution)/shard_map/pallas_call | solution.py:211
  21.2 1.9 %collective-permute-start.5 = (bf16[2048,128]{1,0:T(8,128)(2,1)S(1)}, bf16[2048,128]{1,0:T(8,128)(2,1)S(1)}, u32[]{:S(2)}, u32[]{:S(2)}) collective-permute-start(bf16[2048,128]{1,0:T(8,128)(2,1)S(1)} %get-tuple-element.36.refs_2_), channel_id=1, source_target_pairs={{0,1},{1,0},{2,3},{3,2},{4,5},{5,4},{6,7},{7,6},{8,9},{9,8},{10,11... | collective-permute-start | bytes 1572872 | tf_op jit(solution)/shard_map/ppermute | solution.py:302
  23.1 4.8 %collective-permute-start.6 = (bf16[2048,128]{1,0:T(8,128)(2,1)S(1)}, bf16[2048,128]{1,0:T(8,128)(2,1)S(1)}, u32[]{:S(2)}, u32[]{:S(2)}) collective-permute-start(bf16[2048,128]{1,0:T(8,128)(2,1)S(1)} %get-tuple-element.37.refs_4_), channel_id=1, source_target_pairs={{1,2},{2,1},{3,4},{4,3},{5,6},{6,5},{7,8},{8,7},{9,10},{10,9},{11,... | collective-permute-start | bytes 1572872 | tf_op jit(solution)/shard_map/ppermute | solution.py:303
  28.0 7.8 %toeplitz.1.refs_1_ = bf16[256,256,128]{2,1,0:T(8,128)(2,1)S(1)} custom-call(f32[1,256,128]{2,1,0:T(8,128)} %taps_ref.1), custom_call_target="tpu_custom_call" | custom-call | tf_op jit(solution)/shard_map/toeplitz/pallas_call | solution.py:191
  35.8 0.0 collective-permute-done.1.refs_3_
  35.8 0.0 collective-permute-done.2.refs_5_
  35.8 3.1 %shard_map.57 = (bf16[120,1024]{1,0:T(8,128)(2,1)S(1)}, f32[8,1024]{1,0:T(8,128)S(1)}, f32[8,1024]{1,0:T(8,128)S(1)}) custom-call(s32[1]{0:T(128)} %bitcast.refs_0_, bf16[256,256,128]{2,1,0:T(8,128)(2,1)S(1)} %toeplitz.1.refs_1_, bf16[2048,128]{1,0:T(8,128)(2,1)S(1)} %get-tuple-element.27.refs_2_, bf16[2048,128]{1,0:T(8,128)(2,1)S(1)} %collective-permute-done.1.refs_3_, ...), custom_call_target="tpu_custom_call" | custom-call | tf_op jit(solution)/shard_map/pallas_call | solution.py:242
  38.9 3.1 %shard_map.58 = (bf16[120,1024]{1,0:T(8,128)(2,1)S(1)}, f32[8,1024]{1,0:T(8,128)S(1)}, f32[8,1024]{1,0:T(8,128)S(1)}) custom-call(s32[1]{0:T(128)} %bitcast.refs_0_, bf16[256,256,128]{2,1,0:T(8,128)(2,1)S(1)} %toeplitz.1.refs_1_, bf16[2048,128]{1,0:T(8,128)(2,1)S(1)} %get-tuple-element.27.refs_2_, bf16[2048,128]{1,0:T(8,128)(2,1)S(1)} %collective-permute-done.1.refs_3_, ...), custom_call_target="tpu_custom_call" | custom-call | tf_op jit(solution)/shard_map/pallas_call | solution.py:242
  42.0 0.0 collective-permute-done.5.refs_3_
  42.0 0.0 collective-permute-done.6.refs_5_
  42.0 3.1 %shard_map.59 = (bf16[120,1024]{1,0:T(8,128)(2,1)S(1)}, f32[8,1024]{1,0:T(8,128)S(1)}, f32[8,1024]{1,0:T(8,128)S(1)}) custom-call(s32[1]{0:T(128)} %bitcast.refs_0_, bf16[256,256,128]{2,1,0:T(8,128)(2,1)S(1)} %toeplitz.1.refs_1_, bf16[2048,128]{1,0:T(8,128)(2,1)S(1)} %get-tuple-element.36.refs_2_, bf16[2048,128]{1,0:T(8,128)(2,1)S(1)} %collective-permute-done.5.refs_3_, ...), custom_call_target="tpu_custom_call" | custom-call | tf_op jit(solution)/shard_map/pallas_call | solution.py:242
  45.2 3.1 %shard_map.60 = (bf16[120,1024]{1,0:T(8,128)(2,1)S(1)}, f32[8,1024]{1,0:T(8,128)S(1)}, f32[8,1024]{1,0:T(8,128)S(1)}) custom-call(s32[1]{0:T(128)} %bitcast.refs_0_, bf16[256,256,128]{2,1,0:T(8,128)(2,1)S(1)} %toeplitz.1.refs_1_, bf16[2048,128]{1,0:T(8,128)(2,1)S(1)} %get-tuple-element.36.refs_2_, bf16[2048,128]{1,0:T(8,128)(2,1)S(1)} %collective-permute-done.5.refs_3_, ...), custom_call_target="tpu_custom_call" | custom-call | tf_op jit(solution)/shard_map/pallas_call | solution.py:242
  48.3 2.8 %collective-permute-start.9 = (f32[8,4096]{1,0:T(8,128)S(1)}, f32[8,4096]{1,0:T(8,128)S(1)}, u32[]{:S(2)}, u32[]{:S(2)}) collective-permute-start(f32[8,4096]{1,0:T(8,128)S(1)} %pad_maximum_fusion), channel_id=1, source_target_pairs={{1,0},{2,1},{3,2},{4,3},{5,4},{6,5},{7,6},{8,7},{9,8},{10,9},{11,1... | collective-permute-start | bytes 393224 | tf_op jit(solution)/shard_map/ppermute | solution.py:318
  51.1 18.7 %collective-permute-start.8 = (bf16[120,1024]{1,0:T(8,128)(2,1)S(1)}, bf16[120,1024]{1,0:T(8,128)(2,1)S(1)}, u32[]{:S(2)}, u32[]{:S(2)}) collective-permute-start(bf16[120,1024]{1,0:T(8,128)(2,1)S(1)} %get-tuple-element.43), channel_id=1, source_target_pairs={{0,992},{32,0},{64,32},{96,64},{128,96},{160,128},{192,160},{224,1... | collective-permute-start | bytes 737288 | tf_op jit(solution)/shard_map/ppermute | solution.py:313
  69.8 2.9 %collective-permute-start.7 = (bf16[120,1024]{1,0:T(8,128)(2,1)S(1)}, bf16[120,1024]{1,0:T(8,128)(2,1)S(1)}, u32[]{:S(2)}, u32[]{:S(2)}) collective-permute-start(bf16[120,1024]{1,0:T(8,128)(2,1)S(1)} %get-tuple-element.41), channel_id=1, source_target_pairs={{0,992},{32,0},{64,32},{96,64},{128,96},{160,128},{192,160},{224,1... | collective-permute-start | bytes 737288 | tf_op jit(solution)/shard_map/ppermute | solution.py:313
  72.8 2.9 %collective-permute-start.4 = (bf16[120,1024]{1,0:T(8,128)(2,1)S(1)}, bf16[120,1024]{1,0:T(8,128)(2,1)S(1)}, u32[]{:S(2)}, u32[]{:S(2)}) collective-permute-start(bf16[120,1024]{1,0:T(8,128)(2,1)S(1)} %get-tuple-element.35), channel_id=1, source_target_pairs={{0,992},{32,0},{64,32},{96,64},{128,96},{160,128},{192,160},{224,1... | collective-permute-start | bytes 737288 | tf_op jit(solution)/shard_map/ppermute | solution.py:313
  75.7 2.9 %collective-permute-start.3 = (bf16[120,1024]{1,0:T(8,128)(2,1)S(1)}, bf16[120,1024]{1,0:T(8,128)(2,1)S(1)}, u32[]{:S(2)}, u32[]{:S(2)}) collective-permute-start(bf16[120,1024]{1,0:T(8,128)(2,1)S(1)} %get-tuple-element.33), channel_id=1, source_target_pairs={{0,992},{32,0},{64,32},{96,64},{128,96},{160,128},{192,160},{224,1... | collective-permute-start | bytes 737288 | tf_op jit(solution)/shard_map/ppermute | solution.py:313
  78.6 0.0 collective-permute-done.9
  78.6 4.1 %collective-permute-start.10 = (bf16[8,4096]{1,0:T(8,128)(2,1)S(1)}, bf16[8,4096]{1,0:T(8,128)(2,1)S(1)}, u32[]{:S(2)}, u32[]{:S(2)}) collective-permute-start(bf16[8,4096]{1,0:T(8,128)(2,1)S(1)} %fusion), channel_id=1, source_target_pairs={{0,992},{32,0},{64,32},{96,64},{128,96},{160,128},{192,160},{224,1... | collective-permute-start | bytes 196616 | tf_op jit(solution)/shard_map/ppermute | solution.py:320
  82.8 8.5 %collective-permute-done.3 = bf16[120,1024]{1,0:T(8,128)(2,1)S(1)} collective-permute-done((bf16[120,1024]{1,0:T(8,128)(2,1)S(1)}, bf16[120,1024]{1,0:T(8,128)(2,1)S(1)}, u32[]{:S(2)}, u32[]{:S(2)}) %collective-permute-start.3) | collective-permute-done | bytes 245792 | tf_op jit(solution)/shard_map/ppermute | solution.py:313
  91.3 0.1 pad_bitcast_fusion
  91.4 0.0 collective-permute-done.4
  91.5 0.0 copy-start
  91.5 0.5 collective-permute-done.10
  92.0 0.5 copy-done
  92.5 0.6 bitcast_dynamic-update-slice_fusion.3
  (7 shorter events, 0.1 us)
Async XLA Ops:
  0.8 7.7 %collective-permute-start = (bf16[8,4096]{1,0:T(8,128)(2,1)S(1)}, bf16[8,4096]{1,0:T(8,128)(2,1)S(1)}, u32[]{:S(2)}, u32[]{:S(2)}) collective-permute-start(bf16[8,4096]{1,0:T(8,128)(2,1)S(1)} %slice_bitcast_fusion), channel_id=1, source_target_pairs={{0,1},{1,2},{2,3},{3,4},{4,5},{5,6},{6,7},{7,8},{8,9},{9,10},{10,1... | collective-permute-start | bytes 196616 | tf_op jit(solution)/shard_map/ppermute | solution.py:292
  12.4 23.3 %collective-permute-start.1 = (bf16[2048,128]{1,0:T(8,128)(2,1)S(1)}, bf16[2048,128]{1,0:T(8,128)(2,1)S(1)}, u32[]{:S(2)}, u32[]{:S(2)}) collective-permute-start(bf16[2048,128]{1,0:T(8,128)(2,1)S(1)} %get-tuple-element.27.refs_2_), channel_id=1, source_target_pairs={{0,1},{1,0},{2,3},{3,2},{4,5},{5,4},{6,7},{7,6},{8,9},{9,8},{10,11... | collective-permute-start | bytes 1572872 | tf_op jit(solution)/shard_map/ppermute | solution.py:302
  14.4 21.4 %collective-permute-start.2 = (bf16[2048,128]{1,0:T(8,128)(2,1)S(1)}, bf16[2048,128]{1,0:T(8,128)(2,1)S(1)}, u32[]{:S(2)}, u32[]{:S(2)}) collective-permute-start(bf16[2048,128]{1,0:T(8,128)(2,1)S(1)} %get-tuple-element.28.refs_4_), channel_id=1, source_target_pairs={{1,2},{2,1},{3,4},{4,3},{5,6},{6,5},{7,8},{8,7},{9,10},{10,9},{11,... | collective-permute-start | bytes 1572872 | tf_op jit(solution)/shard_map/ppermute | solution.py:303
  21.2 20.8 %collective-permute-start.5 = (bf16[2048,128]{1,0:T(8,128)(2,1)S(1)}, bf16[2048,128]{1,0:T(8,128)(2,1)S(1)}, u32[]{:S(2)}, u32[]{:S(2)}) collective-permute-start(bf16[2048,128]{1,0:T(8,128)(2,1)S(1)} %get-tuple-element.36.refs_2_), channel_id=1, source_target_pairs={{0,1},{1,0},{2,3},{3,2},{4,5},{5,4},{6,7},{7,6},{8,9},{9,8},{10,11... | collective-permute-start | bytes 1572872 | tf_op jit(solution)/shard_map/ppermute | solution.py:302
  23.1 18.9 %collective-permute-start.6 = (bf16[2048,128]{1,0:T(8,128)(2,1)S(1)}, bf16[2048,128]{1,0:T(8,128)(2,1)S(1)}, u32[]{:S(2)}, u32[]{:S(2)}) collective-permute-start(bf16[2048,128]{1,0:T(8,128)(2,1)S(1)} %get-tuple-element.37.refs_4_), channel_id=1, source_target_pairs={{1,2},{2,1},{3,4},{4,3},{5,6},{6,5},{7,8},{8,7},{9,10},{10,9},{11,... | collective-permute-start | bytes 1572872 | tf_op jit(solution)/shard_map/ppermute | solution.py:303
  48.3 30.3 %collective-permute-start.9 = (f32[8,4096]{1,0:T(8,128)S(1)}, f32[8,4096]{1,0:T(8,128)S(1)}, u32[]{:S(2)}, u32[]{:S(2)}) collective-permute-start(f32[8,4096]{1,0:T(8,128)S(1)} %pad_maximum_fusion), channel_id=1, source_target_pairs={{1,0},{2,1},{3,2},{4,3},{5,4},{6,5},{7,6},{8,7},{9,8},{10,9},{11,1... | collective-permute-start | bytes 393224 | tf_op jit(solution)/shard_map/ppermute | solution.py:318
  51.1 40.3 %collective-permute-start.8 = (bf16[120,1024]{1,0:T(8,128)(2,1)S(1)}, bf16[120,1024]{1,0:T(8,128)(2,1)S(1)}, u32[]{:S(2)}, u32[]{:S(2)}) collective-permute-start(bf16[120,1024]{1,0:T(8,128)(2,1)S(1)} %get-tuple-element.43), channel_id=1, source_target_pairs={{0,992},{32,0},{64,32},{96,64},{128,96},{160,128},{192,160},{224,1... | collective-permute-start | bytes 737288 | tf_op jit(solution)/shard_map/ppermute | solution.py:313
  69.8 21.6 %collective-permute-start.7 = (bf16[120,1024]{1,0:T(8,128)(2,1)S(1)}, bf16[120,1024]{1,0:T(8,128)(2,1)S(1)}, u32[]{:S(2)}, u32[]{:S(2)}) collective-permute-start(bf16[120,1024]{1,0:T(8,128)(2,1)S(1)} %get-tuple-element.41), channel_id=1, source_target_pairs={{0,992},{32,0},{64,32},{96,64},{128,96},{160,128},{192,160},{224,1... | collective-permute-start | bytes 737288 | tf_op jit(solution)/shard_map/ppermute | solution.py:313
  72.8 18.6 %collective-permute-start.4 = (bf16[120,1024]{1,0:T(8,128)(2,1)S(1)}, bf16[120,1024]{1,0:T(8,128)(2,1)S(1)}, u32[]{:S(2)}, u32[]{:S(2)}) collective-permute-start(bf16[120,1024]{1,0:T(8,128)(2,1)S(1)} %get-tuple-element.35), channel_id=1, source_target_pairs={{0,992},{32,0},{64,32},{96,64},{128,96},{160,128},{192,160},{224,1... | collective-permute-start | bytes 737288 | tf_op jit(solution)/shard_map/ppermute | solution.py:313
  75.7 15.6 %collective-permute-start.3 = (bf16[120,1024]{1,0:T(8,128)(2,1)S(1)}, bf16[120,1024]{1,0:T(8,128)(2,1)S(1)}, u32[]{:S(2)}, u32[]{:S(2)}) collective-permute-start(bf16[120,1024]{1,0:T(8,128)(2,1)S(1)} %get-tuple-element.33), channel_id=1, source_target_pairs={{0,992},{32,0},{64,32},{96,64},{128,96},{160,128},{192,160},{224,1... | collective-permute-start | bytes 737288 | tf_op jit(solution)/shard_map/ppermute | solution.py:313
  78.6 13.3 %collective-permute-start.10 = (bf16[8,4096]{1,0:T(8,128)(2,1)S(1)}, bf16[8,4096]{1,0:T(8,128)(2,1)S(1)}, u32[]{:S(2)}, u32[]{:S(2)}) collective-permute-start(bf16[8,4096]{1,0:T(8,128)(2,1)S(1)} %fusion), channel_id=1, source_target_pairs={{0,992},{32,0},{64,32},{96,64},{128,96},{160,128},{192,160},{224,1... | collective-permute-start | bytes 196616 | tf_op jit(solution)/shard_map/ppermute | solution.py:320
  91.5 1.0 %copy-start = (bf16[1,128,4096]{2,1,0:T(8,128)(2,1)}, bf16[1,128,4096]{2,1,0:T(8,128)(2,1)S(1)}, u32[]{:S(2)}) copy-start(bf16[1,128,4096]{2,1,0:T(8,128)(2,1)S(1)} %bitcast_dynamic-update-slice_fusion) | copy-start | bytes 3145732

commit v3 on v2

--- a/solution.py
+++ b/solution.py
@@ -9,6 +9,7 @@
 SHORT = 7
 MEDIUM = 128
 GSIZE = 16
+GROUPS_A_STEP = 64
 LANES = 128
 RIM = 8
 WIDTH = 512
@@ -16,8 +17,8 @@
 
 loss_table = [0.5, 1.0, 1.5, 2.0, 3.0, 0.25, 1.25, 2.5]
 
-HALO_PARTS = (8, 8)
-PASS_PARTS = (4, 4, 4, 4)
+HALO_PARTS = (10, 6)
+PASS_PARTS = (4, 6, 6)
 
 whole = pl.BlockSpec(memory_space=pltpu.VMEM)
 
@@ -54,8 +55,9 @@
 
 def streams_kernel(
     parity_ref, seg_ref, rim_ref, cot_ref, domain_ref, short_ref, after_ref,
-    k_ref, v_ref, first_ref, second_ref, token_ref, weight_ref, x_ref, mixed_ref, grad_ref, *, start,
+    *refs, start,
 ):
+    k_ref, v_ref, first_ref, second_ref, token_ref, weight_ref, x_ref, mixed_ref, grad_ref = refs[-9:]
     step = pl.program_id(0)
     even = parity_ref[0] == 0
 
@@ -63,6 +65,8 @@
     def _():
         weight_ref[...] = token_weights(domain_ref)
         token_ref[...] = jnp.zeros_like(token_ref)
+        if start > 0:
+            first_ref[:start, :] = refs[0][:start, :]
 
     flip = reversal()
     for b in range(seg_ref.shape[2] // LANES):
@@ -89,7 +93,8 @@
         back = jnp.dot(flip, grad_ref[b], preferred_element_type=jnp.float32)
         grad = back.T.astype(jnp.bfloat16)
         out_rows = pl.ds(pl.multiple_of(step * WIDTH + b * LANES, LANES), LANES)
-        first_ref[out_rows, :] = jnp.where(even, mixed, grad)
+        all_rows = pl.ds(pl.multiple_of(start + step * WIDTH + b * LANES, LANES), LANES)
+        first_ref[all_rows, :] = jnp.where(even, mixed, grad)
         second_ref[out_rows, :] = jnp.where(even, grad, mixed)
 
 
@@ -135,10 +140,11 @@
         convs, backs = [], []
         for g in range(per_block):
             at = pl.ds(pl.multiple_of(here + b * LANES + g * GSIZE, GSIZE), GSIZE)
+            full = pl.ds(pl.multiple_of(start + step * width + b * LANES + g * GSIZE, GSIZE), GSIZE)
             windows = jnp.concatenate(
                 [
-                    jnp.concatenate([second_got_ref[at, :], first_ref[at, :]], 1),
-                    jnp.concatenate([first_got_ref[at, :], second_ref[at, :]], 1),
+                    jnp.concatenate([second_got_ref[at, :], first_ref[full, :]], 1),
+                    jnp.concatenate([first_got_ref[full, :], second_ref[at, :]], 1),
                 ],
                 0,
             )
@@ -188,39 +194,47 @@
 
 def toeplitz(taps):
     _, groups, count = taps.shape
+    a_step = min(groups, GROUPS_A_STEP)
     return pl.pallas_call(
         toeplitz_kernel,
         out_shape=pltpu.VMEM((groups, 2 * count, count), jnp.bfloat16),
-        grid=(groups // GSIZE,),
-        in_specs=[pl.BlockSpec((1, GSIZE, count), lambda i: (0, i, 0))],
+        grid=(groups // a_step,),
+        in_specs=[pl.BlockSpec((1, a_step, count), lambda i: (0, i, 0))],
         out_specs=whole,
         compiler_params=pltpu.CompilerParams(vmem_limit_bytes=24 << 20),
         name="toeplitz",
     )(taps)
 
 
-def streams(parity, segment, rim, cotangent, domain, short, after, start, size):
+def streams(parity, segment, rim, cotangent, domain, short, after, shared, start, size):
     first = start // WIDTH
+    blocks = WIDTH // LANES
     wide = pltpu.VMEM((MEDIUM, size), jnp.bfloat16)
     tall = pltpu.VMEM((size, MEDIUM), jnp.bfloat16)
-    blocks = WIDTH // LANES
+    full = pltpu.VMEM((segment.shape[2], MEDIUM), jnp.bfloat16)
+    token = pltpu.VMEM((RIM, LANES), jnp.float32)
 
     def kernel(*refs):
         streams_kernel(*refs, start=start)
 
+    operands = [parity, segment, rim, cotangent, domain, short, after]
+    specs = [
+        pl.BlockSpec(memory_space=pltpu.SMEM),
+        pl.BlockSpec((1, MEDIUM, WIDTH), lambda i: (0, 0, first + i)),
+        whole,
+        pl.BlockSpec((1, MEDIUM, WIDTH), lambda i: (0, 0, first + i)),
+        pl.BlockSpec((1, MEDIUM), lambda i: (0, 0)),
+        pl.BlockSpec((3 * SHORT, 1, WIDTH), lambda i: (0, 0, first + i)),
+        whole,
+    ]
+    if shared is not None:
+        operands.append(shared)
+        specs.append(whole)
     return pl.pallas_call(
         kernel,
-        out_shape=(wide, wide, tall, tall, pltpu.VMEM((RIM, LANES), jnp.float32)),
+        out_shape=(wide, wide, full, tall, token),
         grid=(size // WIDTH,),
-        in_specs=[
-            pl.BlockSpec(memory_space=pltpu.SMEM),
-            pl.BlockSpec((1, MEDIUM, WIDTH), lambda i: (0, 0, first + i)),
-            whole,
-            pl.BlockSpec((1, MEDIUM, WIDTH), lambda i: (0, 0, first + i)),
-            pl.BlockSpec((1, MEDIUM), lambda i: (0, 0)),
-            pl.BlockSpec((3 * SHORT, 1, WIDTH), lambda i: (0, 0, first + i)),
-            whole,
-        ],
+        in_specs=specs,
         out_specs=(whole,) * 5,
         scratch_shapes=[
             pltpu.VMEM((MEDIUM, LANES), jnp.float32),
@@ -229,7 +243,7 @@
             pltpu.VMEM((blocks, MEDIUM, LANES), jnp.bfloat16),
         ],
         compiler_params=pltpu.CompilerParams(vmem_limit_bytes=24 << 20),
-    )(parity, segment, rim, cotangent, domain, short, after)
+    )(*operands)
 
 
 def input_grads(parity, matrices, arrays, cotangent, domain, short, after, start, size, base):
@@ -294,21 +308,21 @@
         in_hbm, (segment, cotangent, short, domain, medium_filters)
     )
     matrices = in_vmem(toeplitz(medium_filters))
-    halos, start, after = [], 0, rim
+    halos, start, after, first = [], 0, rim, None
     for part in HALO_PARTS:
         size = part * unit
-        results = streams(parity, segment, rim, cotangent, domain, short, after, start, size)
+        results = streams(parity, segment, rim, cotangent, domain, short, after, first, start, size)
         k, v, first, second, after = map(in_vmem, results)
-        first_got = in_vmem(lax.ppermute(first, "ctx", inner))
         second_got = in_vmem(lax.ppermute(second, "ctx", outer))
-        halos.append((start, size, (first, first_got, second, second_got, k, v)))
+        halos.append((start, size, (second, second_got, k, v)))
         start += size
+    first_got = in_vmem(lax.ppermute(first, "ctx", inner))
     passed, own, sent, start = [], [], [], 0
     for part in PASS_PARTS:
         size = part * unit
         base, _, arrays = next(h for h in halos if h[0] <= start < h[0] + h[1])
         out, own_part, sent_part = input_grads(
-            parity, matrices, arrays, cotangent, domain, short, after, start, size, base
+            parity, matrices, (first, first_got, *arrays), cotangent, domain, short, after, start, size, base
         )
         passed.append((start, lax.ppermute(out, "pipe", passing)))
         own.append(own_part)

time: 94.1 us -> 89.5 us (0.951)
  waiting for transfers between devices: 14.8 us -> 21.4 us
  starting transfers between devices: 47.8 us -> 41.8 us
  Pallas kernels: 28.1 us -> 23.2 us
    ppermute x4 -> x3, waiting for transfers between devices: 8.51 us -> 12.6 us  [body(): passed.append((start, lax.ppermute(out, 'pipe', passing)))]
    pallas_call x1, Pallas kernels: 7.78 us -> 3.79 us  [toeplitz(): pl.pallas_call(toeplitz_kernel, out_shape=pltpu.VMEM((groups, 2 * count,...]
    ppermute x4 -> x3, starting transfers between devices: 27.4 us -> 24.5 us  [body(): passed.append((start, lax.ppermute(out, 'pipe', passing)))]
    ppermute x2, waiting for transfers between devices: 0.01 us -> 2.53 us  [body(): second_got = in_vmem(lax.ppermute(second, 'ctx', outer))]
    ppermute x2 -> x1, starting transfers between devices: 3.84 us -> 1.92 us  [body(): first_got = in_vmem(lax.ppermute(first, 'ctx', inner))]
    ppermute x1, starting transfers between devices: 4.12 us -> 2.92 us  [body(): last = lax.ppermute(last, 'pipe', passing)]
    pallas_call x4 -> x3, Pallas kernels: 12.4 us -> 11.4 us  [input_grads(): pl.pallas_call(kernel, out_shape=(pltpu.VMEM((MEDIUM - RIM, size), jnp.bf...]
  transfers between devices with their start and end apart: 11 -> 9, of which waited for: 3 -> 4; matrix products, arithmetic and copies ran while one was open for 0% -> 0% of each run, Pallas kernels for 19% -> 12%
where the time goes in v3:
time: 89.5 us; the launch traced here: 88.8 us
  starting transfers between devices  41.8 us (47%)
  Pallas kernels  23.2 us (26%)
  waiting for transfers between devices  21.4 us (24%)
  local copies, waits for them, and re-layouts  2.11 us (2%)
    ppermute x3, starting transfers between devices, body(): passed.append((start, lax.ppermute(out, 'pipe', passing)))  24.5 us
    ppermute x3, waiting for transfers between devices, body(): passed.append((start, lax.ppermute(out, 'pipe', passing)))  12.6 us
    pallas_call x3, Pallas kernels, input_grads(): pl.pallas_call(kernel, out_shape=(pltpu.VMEM((MEDIUM - RIM, size), jnp.bf...  11.4 us
    pallas_call x2, Pallas kernels, streams(): pl.pallas_call(kernel, out_shape=(wide, wide, full, tall, token), grid=(s...  8.1 us
    ppermute x2, starting transfers between devices, body(): second_got = in_vmem(lax.ppermute(second, 'ctx', outer))  7.67 us
    ppermute x1, waiting for transfers between devices, body(): rim = in_vmem(lax.ppermute(segment[0, MEDIUM - RIM:], 'ctx', onward))  5.76 us
    pallas_call x1, Pallas kernels, toeplitz(): pl.pallas_call(toeplitz_kernel, out_shape=pltpu.VMEM((groups, 2 * count,...  3.79 us
    ppermute x1, starting transfers between devices, body(): last = lax.ppermute(last, 'pipe', passing)  2.92 us
  transfers between devices with their start and end apart: 9, of which 4 were waited for; matrix products, arithmetic and copies ran while one was open for 0% of the time, Pallas kernels for 12%

profile of v3, /device:TPU:24, one launch (start us, length us, event | category | flops | bytes accessed | tf_op | source)
XLA Modules:
  0.0 88.8 jit_solution(15693220747588554875)
XLA Ops:
  0.0 0.8 slice_bitcast_fusion
  0.8 1.9 %collective-permute-start = (bf16[8,4096]{1,0:T(8,128)(2,1)S(1)}, bf16[8,4096]{1,0:T(8,128)(2,1)S(1)}, u32[]{:S(2)}, u32[]{:S(2)}) collective-permute-start(bf16[8,4096]{1,0:T(8,128)(2,1)S(1)} %slice_bitcast_fusion), channel_id=1, source_target_pairs={{0,1},{1,2},{2,3},{3,4},{4,5},{5,6},{6,7},{7,8},{8,9},{9,10},{10,1... | collective-permute-start | bytes 196616 | tf_op jit(solution)/shard_map/ppermute | solution.py:306
  2.8 5.8 %collective-permute-done.refs_2_.refs_6_ = bf16[8,4096]{1,0:T(8,128)(2,1)S(1)} collective-permute-done((bf16[8,4096]{1,0:T(8,128)(2,1)S(1)}, bf16[8,4096]{1,0:T(8,128)(2,1)S(1)}, u32[]{:S(2)}, u32[]{:S(2)}) %collective-permute-start) | collective-permute-done | bytes 65568 | tf_op jit(solution)/shard_map/ppermute | solution.py:306
  8.5 4.8 %shard_map.55 = (bf16[128,2560]{1,0:T(8,128)(2,1)S(1)}, bf16[128,2560]{1,0:T(8,128)(2,1)S(1)}, bf16[4096,128]{1,0:T(8,128)(2,1)S(1)}, bf16[2560,128]{1,0:T(8,128)(2,1)S(1)}, f32[8,128]{1,0:T(8,128)S(1)}) custom-call(s32[1]{0:T(128)} %bitcast.refs_0_, bf16[1,128,4096]{2,1,0:T(8,128)(2,1)} %refs_1_.3, ...), custom_call_target="tpu_custom_call" | custom-call | tf_op jit(solution)/shard_map/pallas_call | solution.py:233
  13.4 3.3 %shard_map.56 = (bf16[128,1536]{1,0:T(8,128)(2,1)S(1)}, bf16[128,1536]{1,0:T(8,128)(2,1)S(1)}, bf16[4096,128]{1,0:T(8,128)(2,1)S(1)}, bf16[1536,128]{1,0:T(8,128)(2,1)S(1)}, f32[8,128]{1,0:T(8,128)S(1)}) custom-call(s32[1]{0:T(128)} %bitcast.refs_0_, bf16[1,128,4096]{2,1,0:T(8,128)(2,1)} %refs_1_.3, ...), custom_call_target="tpu_custom_call" | custom-call | tf_op jit(solution)/shard_map/pallas_call | solution.py:233
  16.6 1.9 %collective-permute-start.1 = (bf16[4096,128]{1,0:T(8,128)(2,1)S(1)}, bf16[4096,128]{1,0:T(8,128)(2,1)S(1)}, u32[]{:S(2)}, u32[]{:S(2)}) collective-permute-start(bf16[4096,128]{1,0:T(8,128)(2,1)S(1)} %get-tuple-element.26.refs_2_), channel_id=1, source_target_pairs={{0,1},{1,0},{2,3},{3,2},{4,5},{5,4},{6,7},{7,6},{8,9},{9,8},{10,11... | collective-permute-start | bytes 3145736 | tf_op jit(solution)/shard_map/ppermute | solution.py:319
  18.6 2.8 %collective-permute-start.2 = (bf16[2560,128]{1,0:T(8,128)(2,1)S(1)}, bf16[2560,128]{1,0:T(8,128)(2,1)S(1)}, u32[]{:S(2)}, u32[]{:S(2)}) collective-permute-start(bf16[2560,128]{1,0:T(8,128)(2,1)S(1)} %get-tuple-element.27.refs_4_), channel_id=1, source_target_pairs={{1,2},{2,1},{3,4},{4,3},{5,6},{6,5},{7,8},{8,7},{9,10},{10,9},{11,... | collective-permute-start | bytes 1966088 | tf_op jit(solution)/shard_map/ppermute | solution.py:316
  21.4 4.8 %collective-permute-start.5 = (bf16[1536,128]{1,0:T(8,128)(2,1)S(1)}, bf16[1536,128]{1,0:T(8,128)(2,1)S(1)}, u32[]{:S(2)}, u32[]{:S(2)}) collective-permute-start(bf16[1536,128]{1,0:T(8,128)(2,1)S(1)} %get-tuple-element.34.refs_4_), channel_id=1, source_target_pairs={{1,2},{2,1},{3,4},{4,3},{5,6},{6,5},{7,8},{8,7},{9,10},{10,9},{11,... | collective-permute-start | bytes 1179656 | tf_op jit(solution)/shard_map/ppermute | solution.py:316
  26.3 3.8 %toeplitz.1.refs_1_ = bf16[256,256,128]{2,1,0:T(8,128)(2,1)S(1)} custom-call(f32[1,256,128]{2,1,0:T(8,128)} %taps_ref.1), custom_call_target="tpu_custom_call" | custom-call | tf_op jit(solution)/shard_map/toeplitz/pallas_call | solution.py:198
  30.1 2.5 %collective-permute-done.2.refs_5_ = bf16[2560,128]{1,0:T(8,128)(2,1)S(1)} collective-permute-done((bf16[2560,128]{1,0:T(8,128)(2,1)S(1)}, bf16[2560,128]{1,0:T(8,128)(2,1)S(1)}, u32[]{:S(2)}, u32[]{:S(2)}) %collective-permute-start.2) | collective-permute-done | bytes 655392 | tf_op jit(solution)/shard_map/ppermute | solution.py:316
  32.6 0.0 collective-permute-done.1.refs_3_
  32.6 3.1 %shard_map.57 = (bf16[120,1024]{1,0:T(8,128)(2,1)S(1)}, f32[8,1024]{1,0:T(8,128)S(1)}, f32[8,1024]{1,0:T(8,128)S(1)}) custom-call(s32[1]{0:T(128)} %bitcast.refs_0_, bf16[256,256,128]{2,1,0:T(8,128)(2,1)S(1)} %toeplitz.1.refs_1_, bf16[4096,128]{1,0:T(8,128)(2,1)S(1)} %get-tuple-element.26.refs_2_, bf16[4096,128]{1,0:T(8,128)(2,1)S(1)} %collective-permute-done.1.refs_3_, ...), custom_call_target="tpu_custom_call" | custom-call | tf_op jit(solution)/shard_map/pallas_call | solution.py:256
  35.7 4.2 %shard_map.58 = (bf16[120,1536]{1,0:T(8,128)(2,1)S(1)}, f32[8,1536]{1,0:T(8,128)S(1)}, f32[8,1536]{1,0:T(8,128)S(1)}) custom-call(s32[1]{0:T(128)} %bitcast.refs_0_, bf16[256,256,128]{2,1,0:T(8,128)(2,1)S(1)} %toeplitz.1.refs_1_, bf16[4096,128]{1,0:T(8,128)(2,1)S(1)} %get-tuple-element.26.refs_2_, bf16[4096,128]{1,0:T(8,128)(2,1)S(1)} %collective-permute-done.1.refs_3_, ...), custom_call_target="tpu_custom_call" | custom-call | tf_op jit(solution)/shard_map/pallas_call | solution.py:256
  39.8 0.0 collective-permute-done.5.refs_5_
  39.8 4.1 %shard_map.59 = (bf16[120,1536]{1,0:T(8,128)(2,1)S(1)}, f32[8,1536]{1,0:T(8,128)S(1)}, f32[8,1536]{1,0:T(8,128)S(1)}) custom-call(s32[1]{0:T(128)} %bitcast.refs_0_, bf16[256,256,128]{2,1,0:T(8,128)(2,1)S(1)} %toeplitz.1.refs_1_, bf16[4096,128]{1,0:T(8,128)(2,1)S(1)} %get-tuple-element.26.refs_2_, bf16[4096,128]{1,0:T(8,128)(2,1)S(1)} %collective-permute-done.1.refs_3_, ...), custom_call_target="tpu_custom_call" | custom-call | tf_op jit(solution)/shard_map/pallas_call | solution.py:256
  44.0 2.8 %collective-permute-start.7 = (f32[8,4096]{1,0:T(8,128)S(1)}, f32[8,4096]{1,0:T(8,128)S(1)}, u32[]{:S(2)}, u32[]{:S(2)}) collective-permute-start(f32[8,4096]{1,0:T(8,128)S(1)} %pad_maximum_fusion), channel_id=1, source_target_pairs={{1,0},{2,1},{3,2},{4,3},{5,4},{6,5},{7,6},{8,7},{9,8},{10,9},{11,1... | collective-permute-start | bytes 393224 | tf_op jit(solution)/shard_map/ppermute | solution.py:332
  46.8 18.7 %collective-permute-start.6 = (bf16[120,1536]{1,0:T(8,128)(2,1)S(1)}, bf16[120,1536]{1,0:T(8,128)(2,1)S(1)}, u32[]{:S(2)}, u32[]{:S(2)}) collective-permute-start(bf16[120,1536]{1,0:T(8,128)(2,1)S(1)} %get-tuple-element.38), channel_id=1, source_target_pairs={{0,992},{32,0},{64,32},{96,64},{128,96},{160,128},{192,160},{224,1... | collective-permute-start | bytes 1105928 | tf_op jit(solution)/shard_map/ppermute | solution.py:327
  65.5 2.9 %collective-permute-start.4 = (bf16[120,1536]{1,0:T(8,128)(2,1)S(1)}, bf16[120,1536]{1,0:T(8,128)(2,1)S(1)}, u32[]{:S(2)}, u32[]{:S(2)}) collective-permute-start(bf16[120,1536]{1,0:T(8,128)(2,1)S(1)} %get-tuple-element.33), channel_id=1, source_target_pairs={{0,992},{32,0},{64,32},{96,64},{128,96},{160,128},{192,160},{224,1... | collective-permute-start | bytes 1105928 | tf_op jit(solution)/shard_map/ppermute | solution.py:327
  68.4 2.9 %collective-permute-start.3 = (bf16[120,1024]{1,0:T(8,128)(2,1)S(1)}, bf16[120,1024]{1,0:T(8,128)(2,1)S(1)}, u32[]{:S(2)}, u32[]{:S(2)}) collective-permute-start(bf16[120,1024]{1,0:T(8,128)(2,1)S(1)} %get-tuple-element.31), channel_id=1, source_target_pairs={{0,992},{32,0},{64,32},{96,64},{128,96},{160,128},{192,160},{224,1... | collective-permute-start | bytes 737288 | tf_op jit(solution)/shard_map/ppermute | solution.py:327
  71.4 0.0 collective-permute-done.7
  71.4 2.9 %collective-permute-start.8 = (bf16[8,4096]{1,0:T(8,128)(2,1)S(1)}, bf16[8,4096]{1,0:T(8,128)(2,1)S(1)}, u32[]{:S(2)}, u32[]{:S(2)}) collective-permute-start(bf16[8,4096]{1,0:T(8,128)(2,1)S(1)} %fusion), channel_id=1, source_target_pairs={{0,992},{32,0},{64,32},{96,64},{128,96},{160,128},{192,160},{224,1... | collective-permute-start | bytes 196616 | tf_op jit(solution)/shard_map/ppermute | solution.py:334
  74.3 12.6 %collective-permute-done.3 = bf16[120,1024]{1,0:T(8,128)(2,1)S(1)} collective-permute-done((bf16[120,1024]{1,0:T(8,128)(2,1)S(1)}, bf16[120,1024]{1,0:T(8,128)(2,1)S(1)}, u32[]{:S(2)}, u32[]{:S(2)}) %collective-permute-start.3) | collective-permute-done | bytes 245792 | tf_op jit(solution)/shard_map/ppermute | solution.py:327
  87.0 0.1 pad_bitcast_fusion
  87.1 0.0 collective-permute-done.4
  87.1 0.0 collective-permute-done.6
  87.2 0.0 copy-start
  87.2 0.5 collective-permute-done.8
  87.7 0.5 copy-done
  88.1 0.6 bitcast_dynamic-update-slice_fusion.2
  (4 shorter events, 0.1 us)
Async XLA Ops:
  0.8 7.7 %collective-permute-start = (bf16[8,4096]{1,0:T(8,128)(2,1)S(1)}, bf16[8,4096]{1,0:T(8,128)(2,1)S(1)}, u32[]{:S(2)}, u32[]{:S(2)}) collective-permute-start(bf16[8,4096]{1,0:T(8,128)(2,1)S(1)} %slice_bitcast_fusion), channel_id=1, source_target_pairs={{0,1},{1,2},{2,3},{3,4},{4,5},{5,6},{6,7},{7,8},{8,9},{9,10},{10,1... | collective-permute-start | bytes 196616 | tf_op jit(solution)/shard_map/ppermute | solution.py:306
  16.6 15.9 %collective-permute-start.1 = (bf16[4096,128]{1,0:T(8,128)(2,1)S(1)}, bf16[4096,128]{1,0:T(8,128)(2,1)S(1)}, u32[]{:S(2)}, u32[]{:S(2)}) collective-permute-start(bf16[4096,128]{1,0:T(8,128)(2,1)S(1)} %get-tuple-element.26.refs_2_), channel_id=1, source_target_pairs={{0,1},{1,0},{2,3},{3,2},{4,5},{5,4},{6,7},{7,6},{8,9},{9,8},{10,11... | collective-permute-start | bytes 3145736 | tf_op jit(solution)/shard_map/ppermute | solution.py:319
  18.6 14.0 %collective-permute-start.2 = (bf16[2560,128]{1,0:T(8,128)(2,1)S(1)}, bf16[2560,128]{1,0:T(8,128)(2,1)S(1)}, u32[]{:S(2)}, u32[]{:S(2)}) collective-permute-start(bf16[2560,128]{1,0:T(8,128)(2,1)S(1)} %get-tuple-element.27.refs_4_), channel_id=1, source_target_pairs={{1,2},{2,1},{3,4},{4,3},{5,6},{6,5},{7,8},{8,7},{9,10},{10,9},{11,... | collective-permute-start | bytes 1966088 | tf_op jit(solution)/shard_map/ppermute | solution.py:316
  21.4 18.4 %collective-permute-start.5 = (bf16[1536,128]{1,0:T(8,128)(2,1)S(1)}, bf16[1536,128]{1,0:T(8,128)(2,1)S(1)}, u32[]{:S(2)}, u32[]{:S(2)}) collective-permute-start(bf16[1536,128]{1,0:T(8,128)(2,1)S(1)} %get-tuple-element.34.refs_4_), channel_id=1, source_target_pairs={{1,2},{2,1},{3,4},{4,3},{5,6},{6,5},{7,8},{8,7},{9,10},{10,9},{11,... | collective-permute-start | bytes 1179656 | tf_op jit(solution)/shard_map/ppermute | solution.py:316
  44.0 27.4 %collective-permute-start.7 = (f32[8,4096]{1,0:T(8,128)S(1)}, f32[8,4096]{1,0:T(8,128)S(1)}, u32[]{:S(2)}, u32[]{:S(2)}) collective-permute-start(f32[8,4096]{1,0:T(8,128)S(1)} %pad_maximum_fusion), channel_id=1, source_target_pairs={{1,0},{2,1},{3,2},{4,3},{5,4},{6,5},{7,6},{8,7},{9,8},{10,9},{11,1... | collective-permute-start | bytes 393224 | tf_op jit(solution)/shard_map/ppermute | solution.py:332
  46.8 40.3 %collective-permute-start.6 = (bf16[120,1536]{1,0:T(8,128)(2,1)S(1)}, bf16[120,1536]{1,0:T(8,128)(2,1)S(1)}, u32[]{:S(2)}, u32[]{:S(2)}) collective-permute-start(bf16[120,1536]{1,0:T(8,128)(2,1)S(1)} %get-tuple-element.38), channel_id=1, source_target_pairs={{0,992},{32,0},{64,32},{96,64},{128,96},{160,128},{192,160},{224,1... | collective-permute-start | bytes 1105928 | tf_op jit(solution)/shard_map/ppermute | solution.py:327
  65.5 21.5 %collective-permute-start.4 = (bf16[120,1536]{1,0:T(8,128)(2,1)S(1)}, bf16[120,1536]{1,0:T(8,128)(2,1)S(1)}, u32[]{:S(2)}, u32[]{:S(2)}) collective-permute-start(bf16[120,1536]{1,0:T(8,128)(2,1)S(1)} %get-tuple-element.33), channel_id=1, source_target_pairs={{0,992},{32,0},{64,32},{96,64},{128,96},{160,128},{192,160},{224,1... | collective-permute-start | bytes 1105928 | tf_op jit(solution)/shard_map/ppermute | solution.py:327
  68.4 18.5 %collective-permute-start.3 = (bf16[120,1024]{1,0:T(8,128)(2,1)S(1)}, bf16[120,1024]{1,0:T(8,128)(2,1)S(1)}, u32[]{:S(2)}, u32[]{:S(2)}) collective-permute-start(bf16[120,1024]{1,0:T(8,128)(2,1)S(1)} %get-tuple-element.31), channel_id=1, source_target_pairs={{0,992},{32,0},{64,32},{96,64},{128,96},{160,128},{192,160},{224,1... | collective-permute-start | bytes 737288 | tf_op jit(solution)/shard_map/ppermute | solution.py:327
  71.4 16.3 %collective-permute-start.8 = (bf16[8,4096]{1,0:T(8,128)(2,1)S(1)}, bf16[8,4096]{1,0:T(8,128)(2,1)S(1)}, u32[]{:S(2)}, u32[]{:S(2)}) collective-permute-start(bf16[8,4096]{1,0:T(8,128)(2,1)S(1)} %fusion), channel_id=1, source_target_pairs={{0,992},{32,0},{64,32},{96,64},{128,96},{160,128},{192,160},{224,1... | collective-permute-start | bytes 196616 | tf_op jit(solution)/shard_map/ppermute | solution.py:334
  87.2 1.0 %copy-start = (bf16[1,128,4096]{2,1,0:T(8,128)(2,1)}, bf16[1,128,4096]{2,1,0:T(8,128)(2,1)S(1)}, u32[]{:S(2)}) copy-start(bf16[1,128,4096]{2,1,0:T(8,128)(2,1)S(1)} %bitcast_dynamic-update-slice_fusion) | copy-start | bytes 3145732
